TPU v7x, 256 devices: a whole 4x4x8 slice. The times are simulated.
256 devices in a mesh: dp: 8 (over z), label: 32 (over y, x, core).
Axes of the slice: x: 4, y: 4, z: 8, core: 2. Of those that a mesh axis runs over, the one named last changes fastest.
Arguments:
- enc: bfloat16 [262144, 768], P(('dp', 'label')), may hold values from -6 to 6
- proj: bfloat16 [768, 768], replicated, may hold values from -0.21875 to 0.21875
- head_weight: bfloat16 [4096, 768], P('label'), may hold values from -0.21875 to 0.21875
- shortlist: int32 [2048, 4], P(('dp', 'label')), may hold values from 0 to 31, all different within a row; in each aligned block of 8 rows (0 to 7, 8 to 15, ...) at most 2 rows name the same one
- positives: int32 [262144, 8], P(('dp', 'label')), may hold values from 0 to 511
- weight_num: int32 [4096], P('label'), may hold values from 1 to 16
- weight_den: int32 [4096], P('label'), may hold values from 1 to 16
Outputs:
- grad_enc: float32 [262144, 768], P(('dp', 'label'))
- grad_proj: float32 [768, 768], replicated
- grad_head: float32 [4096, 768], P('label', 'dp')
Inputs may be any that keep to these rules, and one draw needn't show every extreme that they name: `shortlist`: each row names 4 different clusters; among the rows of one device no cluster is named by more than 2 rows, and in every draw some cluster is named by exactly 2 rows of some device; every cluster is named somewhere.
All inputs are finite; a program needn't handle non-finite values.
Results may differ from a plain program's by a relative error of at most 0.005.
Values may be sent and summed in bfloat16 or wider, within the bound.
A program may use at most 128 MiB of HBM per device.

v0:
```python
import jax
import jax.numpy as jnp
from jax import lax
from jax.sharding import PartitionSpec as P


def contract(left, right, left_dim, right_dim):
    return lax.dot_general(
        left, right, (((left_dim,), (right_dim,)), ((), ())), preferred_element_type=jnp.float32
    )


def cluster_grads(hidden_rows, cluster_rows, cluster_scale, wanted, keeping):
    cluster_size = cluster_rows.shape[-2]
    sample_block = hidden_rows.shape[1]
    label_iota = jnp.arange(cluster_size, dtype=jnp.int32)
    logits = jnp.einsum(
        "msd,ld->msl", hidden_rows, cluster_rows, preferred_element_type=jnp.float32
    )
    target = jnp.zeros(logits.shape, jnp.bool_)
    for column in range(wanted.shape[2]):
        target = target | (wanted[:, :, column, None] == label_iota)
    scaled = cluster_scale * (jax.nn.sigmoid(logits) - target.astype(jnp.float32)) / sample_block
    grad_logits = (scaled * keeping[:, None, None]).astype(jnp.bfloat16)
    grad_part = jnp.einsum(
        "msl,ld->msd", grad_logits, cluster_rows, preferred_element_type=jnp.float32
    ).astype(jnp.bfloat16)
    grad_cluster = jnp.einsum(
        "msl,msd->ld", grad_logits, hidden_rows, preferred_element_type=jnp.float32
    )
    return (grad_part, grad_cluster)


def shards(enc, proj, head_weight, shortlist, positives, weight_num, weight_den):
    owners = lax.axis_size("label")
    block_count, beam_width = shortlist.shape
    samples, model_width = enc.shape
    sample_block = samples // block_count
    cluster_size = head_weight.shape[0]
    positive_count = positives.shape[1]
    pair_count = block_count * beam_width
    hidden = jnp.dot(enc, proj, preferred_element_type=jnp.float32).astype(jnp.bfloat16)
    hidden_blocks = hidden.reshape(block_count, sample_block, model_width)
    wanted_blocks = positives.reshape(block_count, sample_block, positive_count)
    capacity = max(2, 2 * pair_count // owners)
    slot_count = owners * capacity
    pair_owner = shortlist.reshape(pair_count)
    pair_iota = jnp.arange(pair_count, dtype=jnp.int32)
    earlier = (pair_owner[:, None] == pair_owner[None, :]) & (
        pair_iota[None, :] < pair_iota[:, None]
    )
    pair_rank = jnp.sum(earlier.astype(jnp.int32), axis=1)
    pair_slot = pair_owner * capacity + pair_rank
    slot_iota = jnp.arange(slot_count, dtype=jnp.int32)
    placed = pair_slot[None, :] == slot_iota[:, None]
    occupied = jnp.any(placed, axis=1).astype(jnp.int32)
    source_pair = jnp.sum(jnp.where(placed, pair_iota[None, :], 0), axis=1)
    source_block = source_pair // beam_width
    source_slot = source_pair % beam_width
    send_rows = jnp.take(hidden_blocks, source_block, axis=0)
    send_wanted = (
        jnp.take(wanted_blocks, source_block, axis=0) - (source_slot * cluster_size)[:, None, None]
    )
    recv_rows, recv_wanted, recv_occupied = (
        lax.all_to_all(send_rows, "label", split_axis=0, concat_axis=0, tiled=True),
        lax.all_to_all(send_wanted, "label", split_axis=0, concat_axis=0, tiled=True),
        lax.all_to_all(occupied, "label", split_axis=0, concat_axis=0, tiled=True),
    )
    cluster_scale = weight_num.astype(jnp.float32) / weight_den.astype(jnp.float32)
    grad_part, weight_part = cluster_grads(
        recv_rows, head_weight, cluster_scale, recv_wanted, recv_occupied.astype(jnp.float32)
    )
    returned = lax.all_to_all(grad_part, "label", split_axis=0, concat_axis=0, tiled=True)
    block_pick = jnp.sum(
        placed.reshape(slot_count, block_count, beam_width).astype(jnp.int32), axis=2
    ).T.astype(jnp.bfloat16)
    grad_hidden = jnp.einsum(
        "bm,msd->bsd", block_pick, returned, preferred_element_type=jnp.float32
    )
    grad_hidden = grad_hidden.reshape(samples, model_width).astype(jnp.bfloat16)
    grad_enc = contract(grad_hidden, proj, 1, 1)
    grad_proj = lax.psum(contract(enc, grad_hidden, 0, 0), ("dp", "label"))
    grad_head = lax.psum_scatter(weight_part, "dp", scatter_dimension=1, tiled=True)
    return (grad_enc, grad_proj, grad_head)


def solution(mesh):
    placed = (
        P(("dp", "label"), None),
        P(),
        P("label", None),
        P(("dp", "label"), None),
        P(("dp", "label"), None),
        P("label"),
        P("label"),
    )
    return jax.shard_map(
        shards,
        mesh=mesh,
        in_specs=placed,
        out_specs=(P(("dp", "label"), None), P(), P("label", "dp")),
        check_vma=False,
    )
```

profile of v0, /device:TPU:1, one launch (start us, length us, event | category | flops | bytes accessed | tf_op | source)
XLA Modules:
  0.0 717.3 jit_solution(10684612803308153281)
XLA Ops:
  8.0 0.0 copy-start
  8.0 0.9 copy.28
  8.9 0.1 eq.157
  9.0 0.2 convert_reduce_fusion.1
  9.2 0.1 fusion.15
  9.3 0.7 reshape.137
  10.0 8.6 %all-to-all-start.2 = ((s32[32,2,1]{1,2,0:T(1,128)}), s32[32,2,1]{1,2,0:T(1,128)S(1)}, u32[]{:S(2)}, u32[]{:S(2)}) async-start(s32[32,2,1]{1,2,0:T(1,128)} %bitcast.14), calls=%async_computation.2 | async-start | bytes 32768 | tf_op jit(solution)/shard_map/all_to_all | solution.py:67
  18.6 0.1 select_reduce_fusion
  18.7 1.4 gather_fusion.1
  20.1 0.0 copy-done
  20.1 2.7 convolution_convert_fusion.1
  22.8 0.9 select_subtract_fusion
  23.7 7.0 gather_fusion
  30.7 0.0 all-to-all-done.2
  30.7 7.4 %all-to-all-start.1 = ((s32[64,128,8]{1,2,0:T(8,128)}), s32[64,128,8]{1,2,0:T(8,128)S(1)}, u32[]{:S(2)}, u32[]{:S(2)}) async-start(s32[64,128,8]{1,2,0:T(8,128)} %select_subtract_fusion), calls=%async_computation.1 | async-start | bytes 524288 | tf_op jit(solution)/shard_map/all_to_all | solution.py:66
  38.1 10.9 %broadcast_select_fusion = bf16[64,128,768]{2,1,0:T(8,128)(2,1)} fusion(bf16[64,128,768]{2,1,0:T(8,128)(2,1)} %gather_fusion, pred[64]{0:T(512)(128)(4,1)S(1)} %compare_and_fusion), kind=kLoop, calls=%fused_computation.4 | loop fusion | flops 6291456 | bytes 25165888 | tf_op jit(solution)/shard_map/jit(_take)/select_n | solution.py:60
  49.0 0.0 copy-start.2
  49.0 0.0 copy-start.3
  49.0 0.0 copy-start.1
  49.0 0.0 all-to-all-done.1
  49.0 8.2 %all-to-all-start = ((bf16[64,128,768]{2,1,0:T(8,128)(2,1)}), bf16[64,128,768]{2,1,0:T(8,128)(2,1)}, u32[]{:S(2)}, u32[]{:S(2)}) async-start(bf16[64,128,768]{2,1,0:T(8,128)(2,1)} %broadcast_select_fusion), calls=%async_computation | async-start | bytes 25165824 | tf_op jit(solution)/shard_map/all_to_all | solution.py:65
  57.2 0.0 copy-done.2
  57.3 0.0 copy-done.3
  57.3 0.1 multiply_reduce_fusion
  57.3 0.1 mul.57
  57.4 0.2 fusion.21
  57.6 151.5 %all-to-all-done = bf16[64,128,768]{2,1,0:T(8,128)(2,1)} async-done(((bf16[64,128,768]{2,1,0:T(8,128)(2,1)}), bf16[64,128,768]{2,1,0:T(8,128)(2,1)}, u32[]{:S(2)}, u32[]{:S(2)}) %all-to-all-start) | async-done | bytes 12582944 | tf_op jit(solution)/shard_map/all_to_all | solution.py:65
  209.1 0.0 copy-done.1
  209.1 12.7 %multiply_convert_fusion = bf16[64,128,128]{2,1,0:T(8,128)(2,1)} fusion(bf16[64,128,768]{2,1,0:T(8,128)(2,1)} %all-to-all-done, f32[64]{0:T(128)S(1)} %mul.57, s32[64,128]{1,0:T(8,128)S(1)} %bitcast.50, s32[64,128]{1,0:T(8,128)S(1)} %bitcast.51, s32[64,128]{1,0:T(8,128)S(1)} %bitcast.52, s32[64,128]{1,0:T(8,128)S(1)} %bitcast.53, ...), kind=kOutput, calls=%fused_computation.6 | convolution fusion | flops 1634729984 | bytes 15139584 | tf_op jit(solution)/shard_map/msd,ld->msl/dot_general | solution.py:17
  221.8 6.3 convolution_convert_fusion
  228.1 22.9 %copy.33 = bf16[64,128,768]{2,1,0:T(8,128)(2,1)} copy(bf16[64,128,768]{2,0,1:T(8,128)(2,1)S(1)} %convolution_convert_fusion) | data formatting | bytes 25165824 | tf_op jit(solution)/shard_map/convert_element_type | solution.py:27
  251.1 13.5 %all-to-all-start.3 = ((bf16[64,128,768]{2,1,0:T(8,128)(2,1)}), bf16[64,128,768]{2,1,0:T(8,128)(2,1)}, u32[]{:S(2)}, u32[]{:S(2)}) async-start(bf16[64,128,768]{2,1,0:T(8,128)(2,1)} %copy.33), calls=%async_computation.3 | async-start | bytes 25165824 | tf_op jit(solution)/shard_map/all_to_all | solution.py:73
  264.5 0.2 all-reduce.2.cloned.1.call-start
  264.8 0.1 reduce_sum.32
  264.9 0.1 copy.30
  264.9 0.1 convert_reduce_fusion
  265.0 151.1 %all-to-all-done.3 = bf16[64,128,768]{2,1,0:T(8,128)(2,1)} async-done(((bf16[64,128,768]{2,1,0:T(8,128)(2,1)}), bf16[64,128,768]{2,1,0:T(8,128)(2,1)}, u32[]{:S(2)}, u32[]{:S(2)}) %all-to-all-start.3) | async-done | bytes 12582944 | tf_op jit(solution)/shard_map/all_to_all | solution.py:73
  416.1 18.0 %fusion.10 = bf16[8,128,768]{2,0,1:T(8,128)(2,1)S(1)} fusion(bf16[64,128,768]{2,1,0:T(8,128)(2,1)} %all-to-all-done.3, s32[64,8]{0,1:T(8,128)S(1)} %convert_reduce_fusion), kind=kOutput, calls=%fused_computation.24 | convolution fusion | flops 101450240 | bytes 14157824 | tf_op jit(solution)/shard_map/bm,msd->bsd/dot_general | solution.py:77
  434.1 0.3 copy.35
  434.4 2.8 convolution_bitcast_fusion
  437.3 0.0 all-reduce.2.cloned.1.call-update
  437.3 0.0 reduce-scatter.2.cloned.1.call-start
  437.3 10.9 %convolution_bitcast_fusion.1 = f32[128,768]{0,1:T(8,128)} fusion(bf16[64,128,128]{2,1,0:T(8,128)(2,1)} %multiply_convert_fusion, bf16[64,128,768]{2,1,0:T(8,128)(2,1)} %all-to-all-done), kind=kOutput, calls=%fused_computation.26 | convolution fusion | flops 1610612736 | bytes 15073280 | tf_op jit(solution)/shard_map/msl,msd->ld/dot_general | solution.py:28
  448.3 0.0 reduce-scatter.2.cloned.1.call-update
  448.3 4.4 fusion.22
  452.7 253.9 %all-reduce.2.cloned.1.call-done = f32[768,768]{0,1:T(8,128)} async-done(((f32[768,768]{0,1:T(8,128)}), f32[768,768]{0,1:T(8,128)}) %all-reduce.2.cloned.1.call-update) | async-done | bytes 2359312 | tf_op jit(solution)/shard_map/psum | solution.py:82
  706.5 3.0 copy.37
  709.6 0.0 reduce-scatter.2.cloned.1.call-done
  (8 shorter events, 0.1 us)
Async XLA Ops:
  8.0 12.1 %copy-start = (bf16[1024,768]{1,0:T(8,128)(2,1)S(1)}, bf16[1024,768]{1,0:T(8,128)(2,1)}, u32[]{:S(2)}) copy-start(bf16[1024,768]{1,0:T(8,128)(2,1)} %param.7) | copy-start | bytes 4718596
  10.0 20.7 %all-to-all-start.2 = ((s32[32,2,1]{1,2,0:T(1,128)}), s32[32,2,1]{1,2,0:T(1,128)S(1)}, u32[]{:S(2)}, u32[]{:S(2)}) async-start(s32[32,2,1]{1,2,0:T(1,128)} %bitcast.14), calls=%async_computation.2 | async-start | bytes 32768 | tf_op jit(solution)/shard_map/all_to_all | solution.py:67
  30.7 18.4 %all-to-all-start.1 = ((s32[64,128,8]{1,2,0:T(8,128)}), s32[64,128,8]{1,2,0:T(8,128)S(1)}, u32[]{:S(2)}, u32[]{:S(2)}) async-start(s32[64,128,8]{1,2,0:T(8,128)} %select_subtract_fusion), calls=%async_computation.1 | async-start | bytes 524288 | tf_op jit(solution)/shard_map/all_to_all | solution.py:66
  49.0 8.2 %copy-start.2 = (s32[128]{0:T(128)S(1)}, s32[128]{0:T(128)}, u32[]{:S(2)}) copy-start(s32[128]{0:T(128)} %param.13) | copy-start | bytes 1540
  49.0 8.2 %copy-start.3 = (s32[128]{0:T(128)S(1)}, s32[128]{0:T(128)}, u32[]{:S(2)}) copy-start(s32[128]{0:T(128)} %param.12) | copy-start | bytes 1540
  49.0 160.1 %copy-start.1 = (bf16[128,768]{1,0:T(8,128)(2,1)S(1)}, bf16[128,768]{1,0:T(8,128)(2,1)}, u32[]{:S(2)}) copy-start(bf16[128,768]{1,0:T(8,128)(2,1)} %param.9) | copy-start | bytes 589828
  49.0 160.1 %all-to-all-start = ((bf16[64,128,768]{2,1,0:T(8,128)(2,1)}), bf16[64,128,768]{2,1,0:T(8,128)(2,1)}, u32[]{:S(2)}, u32[]{:S(2)}) async-start(bf16[64,128,768]{2,1,0:T(8,128)(2,1)} %broadcast_select_fusion), calls=%async_computation | async-start | bytes 25165824 | tf_op jit(solution)/shard_map/all_to_all | solution.py:65
  251.1 165.1 %all-to-all-start.3 = ((bf16[64,128,768]{2,1,0:T(8,128)(2,1)}), bf16[64,128,768]{2,1,0:T(8,128)(2,1)}, u32[]{:S(2)}, u32[]{:S(2)}) async-start(bf16[64,128,768]{2,1,0:T(8,128)(2,1)} %copy.33), calls=%async_computation.3 | async-start | bytes 25165824 | tf_op jit(solution)/shard_map/all_to_all | solution.py:73
  264.5 442.0 %all-reduce.2.cloned.1.call-start = ((), (), s32[]{:S(2)}) async-start(), calls=%async_computation.5 | async-start | bytes 4718592 | tf_op jit(solution)/shard_map/psum | solution.py:82
  437.3 272.3 %reduce-scatter.2.cloned.1.call-start = ((), (), s32[]{:S(2)}) async-start(), calls=%async_computation.6 | async-start | bytes 442368 | tf_op jit(solution)/shard_map/reduce_scatter | solution.py:83
Sparse Core Ops, SparseCore 0:
  437.4 269.0 all-reduce.1
Sparse Core Ops, SparseCore 1:
  448.4 39.7 reduce-scatter.1
where the time goes:
time: 723 us; the launch traced here: 717 us
  waiting for transfers between devices  557 us (77%)
  matrix products  57.8 us (8%)
  starting transfers between devices  38 us (5%)
  local copies, waits for them, and re-layouts  36.7 us (5%)
  between operations  15.9 us (2%)
  other arithmetic  12.4 us (2%)
    psum x1, waiting for transfers between devices, shards(): grad_proj = lax.psum(contract(enc, grad_hidden, 0, 0), ('dp', 'label'))  254 us
    all_to_all x1, waiting for transfers between devices, shards(): lax.all_to_all(send_rows, 'label', split_axis=0, concat_axis=0, tiled=True)  151 us
    all_to_all x1, waiting for transfers between devices, shards(): lax.all_to_all(grad_part, 'label', split_axis=0, concat_axis=0, tiled=True)  151 us
    convert_element_type x1, local copies, waits for them, and re-layouts, cluster_grads(): grad_part = jnp.einsum('msl,ld->msd', grad_logits, cluster_rows, preferre...  22.9 us
    dot_general x1, matrix products, shards(): jnp.einsum('bm,msd->bsd', block_pick, returned, preferred_element_type=jn...  18 us
  transfers between devices with their start and end apart: 6, of which 3 were waited for; matrix products, arithmetic and copies ran while one was open for 6% of the time, Pallas kernels for 0%

commit v1 on v0

v1 whole, which is shorter than its diff:
```python
import jax
import jax.numpy as jnp
from jax import lax
from jax.sharding import PartitionSpec as P


def shards(enc, proj, head_weight, shortlist, positives, weight_num, weight_den):
    block_count, beam_width = shortlist.shape
    samples, width = enc.shape
    rows = samples // block_count
    size = head_weight.shape[0]
    clusters = lax.axis_size("label")
    weights = lax.all_gather(head_weight, "label")
    scale = weight_num.astype(jnp.float32) / weight_den.astype(jnp.float32)
    scales = lax.all_gather(scale, "label")
    hidden = jnp.dot(enc, proj, preferred_element_type=jnp.float32).astype(jnp.bfloat16)
    blocks = hidden.reshape(block_count, rows, width)
    picked = jnp.take(weights, shortlist.reshape(-1), axis=0).reshape(
        block_count, beam_width * size, width
    )
    picked_scale = jnp.take(scales, shortlist.reshape(-1), axis=0).reshape(
        block_count, 1, beam_width * size
    )
    logits = jnp.einsum("bsd,bld->bsl", blocks, picked, preferred_element_type=jnp.float32)
    place = jnp.arange(beam_width * size, dtype=jnp.int32)
    wanted = positives.reshape(block_count, rows, -1)
    target = jnp.zeros(logits.shape, jnp.bool_)
    for column in range(wanted.shape[2]):
        target = target | (wanted[:, :, column, None] == place)
    grad_logits = (
        picked_scale * (jax.nn.sigmoid(logits) - target.astype(jnp.float32)) / rows
    ).astype(jnp.bfloat16)
    grad_hidden = jnp.einsum(
        "bsl,bld->bsd", grad_logits, picked, preferred_element_type=jnp.float32
    ).astype(jnp.bfloat16).reshape(samples, width)
    grad_pair = jnp.einsum(
        "bsl,bsd->bld", grad_logits, blocks, preferred_element_type=jnp.float32
    ).astype(jnp.bfloat16).reshape(block_count * beam_width, size, width)
    chosen = (shortlist.reshape(1, -1) == jnp.arange(clusters, dtype=jnp.int32)[:, None]).astype(
        jnp.bfloat16
    )
    grad_all = jnp.einsum("cp,pld->cld", chosen, grad_pair, preferred_element_type=jnp.float32)
    grad_enc = lax.dot_general(
        grad_hidden, proj, (((1,), (1,)), ((), ())), preferred_element_type=jnp.float32
    )
    grad_proj = lax.psum(
        lax.dot_general(
            enc, grad_hidden, (((0,), (0,)), ((), ())), preferred_element_type=jnp.float32
        ),
        ("dp", "label"),
    )
    grad_rows = lax.psum_scatter(grad_all, "label", scatter_dimension=0, tiled=False)
    grad_head = lax.psum_scatter(grad_rows, "dp", scatter_dimension=1, tiled=True)
    return (grad_enc, grad_proj, grad_head)


def solution(mesh):
    placed = (
        P(("dp", "label"), None),
        P(),
        P("label", None),
        P(("dp", "label"), None),
        P(("dp", "label"), None),
        P("label"),
        P("label"),
    )
    return jax.shard_map(
        shards,
        mesh=mesh,
        in_specs=placed,
        out_specs=(P(("dp", "label"), None), P(), P("label", "dp")),
        check_vma=False,
    )
```

time: 723 us -> 538 us (0.74)
  waiting for transfers between devices: 557 us -> 425 us
  starting transfers between devices: 38 us -> 0.16 us
  matrix products: 57.8 us -> 33.1 us
  blocking collectives: 0 us -> 23.2 us
    all_to_all x4 -> x0, waiting for transfers between devices: 303 us -> none  [the longest x1 151 us: shards(): lax.all_to_all(send_rows, 'label', split_axis=0, concat_axis=0, tiled=True)]
    reduce_scatter x1, waiting for transfers between devices: 0.01 us -> 98.6 us  [shards(): lax.psum_scatter(grad_all, 'label', scatter_dimension=0, tiled=False)]
    all_to_all x4 -> x0, starting transfers between devices: 37.7 us -> none  [the longest x1 13.5 us: shards(): lax.all_to_all(grad_part, 'label', split_axis=0, concat_axis=0, tiled=True)]
    unnamed x2 -> x5, waiting for transfers between devices: 0.03 us -> 33.4 us
    all_gather x0 -> x1, waiting for transfers between devices: none -> 30.8 us  [shards(): weights = lax.all_gather(head_weight, 'label')]
    dot_general x6, matrix products: 55.1 us -> 30.4 us  [the longest x1 9.95 us: shards(): jnp.einsum('cp,pld->cld', chosen, grad_pair, preferred_element_type=jnp.f...]
    convert_element_type x3 -> x0, local copies, waits for them, and re-layouts: 23.9 us -> none  [the longest x1 22.9 us: cluster_grads(): grad_part = jnp.einsum('msl,ld->msd', grad_logits, cluster_rows, preferre...]
    all_gather x0 -> x1, blocking collectives: none -> 23.2 us  [shards(): scales = lax.all_gather(scale, 'label')]
  transfers between devices with their start and end apart: 6 -> 4, of which waited for: 3 -> 4; matrix products, arithmetic and copies ran while one was open for 6% -> 5% of each run, Pallas kernels for 0% -> 0%
where the time goes in v1:
time: 538 us; the launch traced here: 533 us
  waiting for transfers between devices  425 us (79%)
  matrix products  33.1 us (6%)
  local copies, waits for them, and re-layouts  32.3 us (6%)
  blocking collectives  23.2 us (4%)
  between operations  13.9 us (3%)
  other arithmetic  5.38 us (1%)
    psum x1, waiting for transfers between devices, shards(): lax.psum(lax.dot_general(enc, grad_hidden, (((0,), (0,)), ((), ())), pref...  262 us
    reduce_scatter x1, waiting for transfers between devices, shards(): lax.psum_scatter(grad_all, 'label', scatter_dimension=0, tiled=False)  98.6 us
    unnamed x5, waiting for transfers between devices  33.4 us
    all_gather x1, waiting for transfers between devices, shards(): weights = lax.all_gather(head_weight, 'label')  30.8 us
    all_gather x1, blocking collectives, shards(): scales = lax.all_gather(scale, 'label')  23.2 us
    dot_general x1, local copies, waits for them, and re-layouts, shards(): jnp.einsum('cp,pld->cld', chosen, grad_pair, preferred_element_type=jnp.f...  16.6 us
  transfers between devices with their start and end apart: 4, of which 4 were waited for; matrix products, arithmetic and copies ran while one was open for 5% of the time, Pallas kernels for 0%

profile of v1, /device:TPU:1, one launch (start us, length us, event | category | flops | bytes accessed | tf_op | source)
XLA Modules:
  0.0 533.3 jit_solution(11376284213874972979)
XLA Ops:
  7.2 0.0 copy-start
  7.2 0.0 all-gather.5.cloned.1.call-start
  7.2 0.7 all-gather.5.cloned.1.call-update
  7.9 0.0 reduce-scatter.5.cloned.1.call-start
  8.0 0.8 copy.40
  8.7 0.1 reshape.83
  8.8 0.1 reshape.79
  8.9 0.7 fusion.21
  9.6 23.2 %all-gather.2 = f32[32,1,128]{2,1,0:T(1,128)S(1)} all-gather(f32[1,1,128]{2,1,0:T(1,128)S(1)} %fusion.21), channel_id=2, replica_groups=mesh['dp'=8,'label'=32] {'label'}, dimensions={0}, use_global_device_ids=true | all-gather | bytes 16896 | tf_op jit(solution)/shard_map/all_gather | solution.py:15
  32.7 0.6 gather_fusion
  33.3 0.7 compare_and_fusion
  34.0 0.1 broadcast_bitcast_fusion
  34.1 0.1 broadcast_select_fusion
  34.2 1.1 fusion.28
  35.2 0.0 copy-done
  35.2 2.7 convolution_convert_fusion.1
  37.9 30.8 %all-gather.5.cloned.1.call-done = bf16[4096,768]{1,0:T(8,128)(2,1)} async-done(((bf16[128,768]{1,0:T(8,128)(2,1)}), bf16[4096,768]{1,0:T(8,128)(2,1)}) %all-gather.5.cloned.1.call-update) | async-done | bytes 6291472 | tf_op jit(solution)/shard_map/all_gather | solution.py:13
  68.7 6.4 %gather_fusion.1 = bf16[32,128,768]{2,1,0:T(8,128)(2,1)} fusion(bf16[32,128,768]{2,1,0:T(8,128)(2,1)} %bitcast.59, s32[1024]{0:T(1024)S(1)} %pad_clamp_fusion), kind=kCustom, calls=%fused_computation.1 | custom fusion | bytes 12583040 | tf_op jit(solution)/shard_map/jit(_take)/gather | solution.py:18
  75.1 3.9 bitcast_select_fusion
  79.0 0.0 copy-start.1
  79.0 2.1 fusion.29
  81.1 0.6 copy-done.1
  81.7 0.0 copy-start.2
  81.7 5.3 convolution_convert_fusion
  87.0 0.0 copy-done.2
  87.0 10.0 %fusion = f32[32,128,768]{2,0,1:T(8,128)} fusion(bf16[32,128,768]{2,1,0:T(8,128)(2,1)S(1)} %bitcast.60, s32[32]{0:T(128)S(1)} %reshape.83), kind=kOutput, calls=%fused_computation.3 | convolution fusion | flops 201327616 | bytes 18874496 | tf_op jit(solution)/shard_map/cp,pld->cld/dot_general | solution.py:42
  97.0 16.6 %copy.52 = f32[32,128,768]{2,1,0:T(8,128)} copy(f32[32,128,768]{2,0,1:T(8,128)} %fusion) | data formatting | bytes 25165824 | tf_op jit(solution)/shard_map/cp,pld->cld/dot_general | solution.py:42
  113.6 0.0 reduce-scatter.5.cloned.1.call-update
  113.6 0.0 all-reduce.2.cloned.1.call-start
  113.6 5.8 %fusion.10 = bf16[8,128,768]{2,1,0:T(8,128)(2,1)S(1)} fusion(bf16[8,512,768]{2,1,0:T(8,128)(2,1)} %copy-done.1, f32[8,128,512]{2,1,0:T(8,128)} %copy-done.2, f32[8,512]{1,0:T(8,128)S(1)} %broadcast_select_fusion, s32[8,128]{1,0:T(8,128)S(1)} %bitcast.82, s32[8,128]{1,0:T(8,128)S(1)} %bitcast.70, s32[8,128]{1,0:T(8,128)S(1)} %bitcast.72, ...), kind=kOutput, calls=%fused_computation.24 | convolution fusion | flops 818151424 | bytes 10010624 | tf_op jit(solution)/shard_map/bsl,bld->bsd/dot_general | solution.py:33
  119.4 0.0 copy-start.4
  119.4 1.2 copy-done.4
  120.6 2.9 convolution_bitcast_fusion
  123.5 0.0 copy-start.3
  123.5 0.0 all-reduce.2.cloned.1.call-update
  123.5 0.0 reduce-scatter.7.cloned.1.call-start
  123.5 98.6 %reduce-scatter.5.cloned.1.call-done = f32[1,128,768]{2,1,0:T(8,128)} async-done(((f32[32,128,768]{2,1,0:T(8,128)}), f32[1,128,768]{2,1,0:T(8,128)}) %reduce-scatter.5.cloned.1.call-update) | async-done | bytes 393232 | tf_op jit(solution)/shard_map/reduce_scatter | solution.py:52
  222.2 1.9 copy.56
  224.1 0.0 reduce-scatter.7.cloned.1.call-update
  224.1 0.0 copy-done.3
  224.1 4.5 fusion.30
  228.6 262.4 %all-reduce.2.cloned.1.call-done = f32[768,768]{0,1:T(8,128)} async-done(((f32[768,768]{0,1:T(8,128)}), f32[768,768]{0,1:T(8,128)}) %all-reduce.2.cloned.1.call-update) | async-done | bytes 2359312 | tf_op jit(solution)/shard_map/psum | solution.py:46
  491.0 3.0 copy.53
  494.1 32.7 %reduce-scatter.7.cloned.1.call-done = f32[96,128]{1,0:T(8,128)} async-done(((f32[768,128]{1,0:T(8,128)}), f32[96,128]{1,0:T(8,128)}) %reduce-scatter.7.cloned.1.call-update) | async-done | bytes 49168
  (3 shorter events, 0.0 us)
Async XLA Ops:
  7.2 28.1 %copy-start = (bf16[1024,768]{1,0:T(8,128)(2,1)S(1)}, bf16[1024,768]{1,0:T(8,128)(2,1)}, u32[]{:S(2)}) copy-start(bf16[1024,768]{1,0:T(8,128)(2,1)} %param.7) | copy-start | bytes 4718596
  7.2 61.5 %all-gather.5.cloned.1.call-start = ((), (), s32[]{:S(2)}) async-start(), calls=%async_computation.4 | async-start | bytes 6488064 | tf_op jit(solution)/shard_map/all_gather | solution.py:13
  7.9 214.3 %reduce-scatter.5.cloned.1.call-start = ((), (), s32[]{:S(2)}) async-start(), calls=%async_computation.3 | async-start | bytes 12976128 | tf_op jit(solution)/shard_map/reduce_scatter | solution.py:52
  79.0 2.7 copy-start.1
  81.7 5.3 copy-start.2
  113.6 377.4 %all-reduce.2.cloned.1.call-start = ((), (), s32[]{:S(2)}) async-start(), calls=%async_computation.2 | async-start | bytes 4718592 | tf_op jit(solution)/shard_map/psum | solution.py:46
  119.4 1.2 copy-start.4
  123.5 100.6 %copy-start.3 = (bf16[768,768]{1,0:T(8,128)(2,1)S(1)}, bf16[768,768]{1,0:T(8,128)(2,1)}, u32[]{:S(2)}) copy-start(bf16[768,768]{1,0:T(8,128)(2,1)} %param.8) | copy-start | bytes 3538948
  123.5 403.3 %reduce-scatter.7.cloned.1.call-start = ((), (), s32[]{:S(2)}) async-start(), calls=%async_computation.5 | async-start | bytes 442368
Sparse Core Ops, SparseCore 0:
  10.5 58.1 all-gather.4
  113.7 108.4 reduce-scatter.4
  228.2 262.8 all-reduce.1
  494.0 32.7 reduce-scatter.6

commit v2 on v1

v2 whole, which is shorter than its diff:
```python
import jax
import jax.numpy as jnp
from jax import lax
from jax.experimental import pallas as pl
from jax.experimental.pallas import tpu as pltpu
from jax.sharding import PartitionSpec as P

MESH = pl.DeviceIdType.MESH
F32 = jnp.float32
BF16 = jnp.bfloat16

D = 768
LB = 128
SB = 128
BEAM = 4
NBLK = 8
ROWS = NBLK * SB
SHARD = D + 16
HALF0, HALF1 = 400, 384
NZ = 8
PIECE = 144
ABLK = 4 * PIECE
CORE = 4 * ABLK


def lid(pa, pb, core):
    xx = pa + core * (pb - pa)
    yy = pb + core * (pa - pb)
    return (yy * 4 + xx) * 2 + core


def kernel(
    sl, tab, live, enc, proj, shard, pos,
    ge_out, gp_out, gh_out,
    wl, hid, hidt, enct, w4, gl, gh, ge,
    sb, rb, cb, cf, r1a, r1b, s2p, s2m, r2p, r2m,
    db0, t1a, t1b, u2p, u2m, v2p, v2m, ef, zs, zr,
    ps0, pr0, pf, pa1, p1a, p1b, ps2p, ps2m, pr2p, pr2m,
    pb0, q1a, q1b, qs2p, qs2m, qr2p, qr2m, ez, zp, po,
    ss, rs, ls,
):
    z = lax.axis_index("dp")
    me = lax.axis_index("label")
    core = me % 2
    x = (me // 2) % 4
    y = me // 8
    pa = x + core * (y - x)
    pb = y + core * (x - y)
    other = 1 - core
    ap, am = (pa + 1) % 4, (pa + 3) % 4
    bp, bm = (pb + 1) % 4, (pb + 3) % 4
    a2, b2 = (pa + 2) % 4, (pb + 2) % 4
    sib = {"label": me + 1 - 2 * core}
    to_ap = {"label": lid(ap, pb, core)}
    to_am = {"label": lid(am, pb, core)}
    to_bp = {"label": lid(pa, bp, core)}
    to_bm = {"label": lid(pa, bm, core)}
    to_z = [None] + [{"dp": (z + dz) % NZ} for dz in range(1, NZ)]

    barrier = pltpu.get_barrier_semaphore()
    greeted = [sib, to_ap, to_am, to_bp, to_bm] + to_z[1:]
    for device in greeted:
        pl.semaphore_signal(barrier, inc=1, device_id=device, device_id_type=MESH)
    pl.semaphore_wait(barrier, len(greeted))

    count = [0]
    sent = []

    def take(n=1):
        first = count[0]
        count[0] += n
        return first

    def remote(src, dst, i, device):
        return pltpu.make_async_remote_copy(
            src_ref=src, dst_ref=dst, send_sem=ss.at[i], recv_sem=rs.at[i],
            device_id=device, device_id_type=MESH,
        )

    def send(src, dst, i, device):
        copy = remote(src, dst, i, device)
        copy.start()
        sent.append(copy)

    def landed(dst, i):
        remote(dst, dst, i, sib).wait_recv()

    def hidden_chunk(i):
        rows = enc[pl.ds(256 * i, 256), :]
        value = jnp.dot(rows, proj[...], preferred_element_type=F32).astype(BF16)
        hid[2 * i] = value[:SB]
        hid[2 * i + 1] = value[SB:]
        hidt[2 * i] = value[:SB].T
        hidt[2 * i + 1] = value[SB:].T
        enct[:, pl.ds(256 * i, 256)] = rows.T

    first = wl.at[pl.ds(0, 1)]
    del first
    own = pltpu.make_async_copy(shard, wl.at[me], ls.at[0])
    own.start()
    top, bottom = pl.ds(0, HALF0), pl.ds(HALF0, HALF1)
    base = take(20)
    near = take(16)

    def slot(a, b):
        return wl.at[lid(a, b, core)]

    columns = [pa, am, ap, a2]
    source = [shard, slot(am, pb), slot(ap, pb), slot(a2, pb)]
    send(shard, wl.at[me], base + 0, to_ap)
    send(shard, wl.at[me], base + 1, to_am)
    send(shard, wl.at[me], base + 4, to_bp)
    send(shard, wl.at[me], base + 5, to_bm)
    send(shard, wl.at[me], near + 0, sib)
    hidden_chunk(0)
    landed(slot(am, pb), base + 0)
    send(slot(am, pb).at[top], slot(am, pb).at[top], base + 2, to_ap)
    send(slot(am, pb), slot(am, pb), base + 8, to_bp)
    send(slot(am, pb), slot(am, pb), base + 9, to_bm)
    send(slot(am, pb), slot(am, pb), near + 1, sib)
    landed(slot(ap, pb), base + 1)
    send(slot(ap, pb).at[bottom], slot(ap, pb).at[bottom], base + 3, to_am)
    send(slot(ap, pb), slot(ap, pb), base + 12, to_bp)
    send(slot(ap, pb), slot(ap, pb), base + 13, to_bm)
    send(slot(ap, pb), slot(ap, pb), near + 2, sib)
    landed(slot(pa, bm), base + 4)
    send(slot(pa, bm).at[top], slot(pa, bm).at[top], base + 6, to_bp)
    send(slot(pa, bm), slot(pa, bm), near + 4, sib)
    landed(slot(pa, bp), base + 5)
    send(slot(pa, bp).at[bottom], slot(pa, bp).at[bottom], base + 7, to_bm)
    send(slot(pa, bp), slot(pa, bp), near + 8, sib)
    hidden_chunk(1)
    landed(slot(a2, pb).at[top], base + 2)
    landed(slot(a2, pb).at[bottom], base + 3)
    send(slot(a2, pb), slot(a2, pb), base + 16, to_bp)
    send(slot(a2, pb), slot(a2, pb), base + 17, to_bm)
    send(slot(a2, pb), slot(a2, pb), near + 3, sib)
    for j in (1, 2, 3):
        a = columns[j]
        landed(slot(a, bm), base + 4 + 4 * j)
        send(slot(a, bm).at[top], slot(a, bm).at[top], base + 6 + 4 * j, to_bp)
        send(slot(a, bm), slot(a, bm), near + 4 + j, sib)
        landed(slot(a, bp), base + 5 + 4 * j)
        send(slot(a, bp).at[bottom], slot(a, bp).at[bottom], base + 7 + 4 * j, to_bm)
        send(slot(a, bp), slot(a, bp), near + 8 + j, sib)
        if j < 3:
            hidden_chunk(1 + j)
    for j in (0, 1, 2, 3):
        a = columns[j]
        landed(slot(a, b2).at[top], base + 6 + 4 * j)
        landed(slot(a, b2).at[bottom], base + 7 + 4 * j)
        send(slot(a, b2), slot(a, b2), near + 12 + j, sib)
    for i in range(16):
        landed(wl.at[0], near + i)
    own.wait()

    place = lax.broadcasted_iota(jnp.int32, (SB, LB), 1)

    def block(b, carry):
        wanted = pos[b]
        for k in range(BEAM):
            c = sl[b * BEAM + k]
            for j in range(D // LB):
                w4[k * LB:(k + 1) * LB, j * LB:(j + 1) * LB] = wl[c, j * LB:(j + 1) * LB, :]
        rows = hid[b]
        parts = []
        for k in range(BEAM):
            c = sl[b * BEAM + k]
            tail = wl[c, D:SHARD, :].astype(F32)
            scale = tail[0:1] / tail[1:2]
            logits = lax.dot_general(
                rows, w4[k * LB:(k + 1) * LB, :], (((1,), (1,)), ((), ())),
                preferred_element_type=F32,
            )
            hit = wanted[:, 0:1] == place + k * LB
            for column in range(1, wanted.shape[1]):
                hit = hit | (wanted[:, column:column + 1] == place + k * LB)
            target = jnp.where(hit, 1.0, 0.0)
            part = (scale * (jax.nn.sigmoid(logits) - target) / SB).astype(BF16)
            gl[b * BEAM + k] = part
            parts.append(part)
        total = jnp.dot(jnp.concatenate(parts, axis=1), w4[...], preferred_element_type=F32)
        gh[pl.ds(pl.multiple_of(b * SB, SB), SB), :] = total.astype(BF16)
        return carry

    lax.fori_loop(0, NBLK, block, 0)

    def proj_half(which):
        lanes = pl.ds(pl.multiple_of(which * (D // 2), 128), D // 2)
        return jnp.dot(enct[...], gh[:, lanes], preferred_element_type=F32)

    value = proj_half(other)
    for j in range(3):
        ps0[j * D:(j + 1) * D, :] = value[:, j * LB:(j + 1) * LB].astype(BF16)

    def cluster(c):
        left = jnp.concatenate([hidt[tab[1, c]], hidt[tab[3, c]]], axis=1)
        one = (gl[tab[0, c]].astype(F32) * live[0, c]).astype(BF16)
        two = (gl[tab[2, c]].astype(F32) * live[1, c]).astype(BF16)
        return jnp.dot(left, jnp.concatenate([one, two], axis=0), preferred_element_type=F32)

    pair0 = take()
    value = proj_half(core)
    send(ps0, pr0, pair0, sib)
    for j in range(3):
        pf[j * D:(j + 1) * D, :] = value[:, j * LB:(j + 1) * LB]

    cross = take(16)

    def across(i):
        return remote(sb.at[i], rb.at[i], cross + i, sib)

    def for_other(i, carry):
        c = lid((pb + 6 - i // 4) % 4, (pa + 6 - i % 4) % 4, other)
        sb[i] = cluster(c).astype(BF16)

        @pl.when(i > 0)
        def _():
            across(i - 1).start()

        return carry

    lax.fori_loop(0, 16, for_other, 0)
    landed(pr0, pair0)
    pf[...] = pf[...] + pr0[...].astype(F32)
    across(15).start()

    def ablk(a):
        return pl.ds(pl.multiple_of(a * ABLK, 16), ABLK)

    pa1[...] = pf[ablk(a2), :].astype(BF16)

    def own_cluster(da, db):
        c = lid((pa + 6 - da) % 4, (pb + 6 - db) % 4, core)
        i = da * 4 + db
        value = cluster(c)
        across(i).wait_recv()
        return value + rb[i].astype(F32)

    def far(db, carry):
        cb[db] = own_cluster(0, db).astype(BF16)
        return carry

    lax.fori_loop(0, 4, far, 0)
    pm1 = take(2)
    send(pa1.at[pl.ds(0, ABLK // 2)], p1a, pm1, to_ap)
    send(pa1.at[pl.ds(ABLK // 2, ABLK // 2)], p1b, pm1 + 1, to_am)

    def nearby(i, carry):
        cf[i] = own_cluster(1 + i // 4, i % 4)
        return carry

    lax.fori_loop(0, 4, nearby, 0)
    m1 = take(8)
    upper, lower = pl.ds(0, D // 2), pl.ds(D // 2, D // 2)
    for db in range(4):
        send(cb.at[db, upper], r1a.at[db], m1 + db, to_ap)
        send(cb.at[db, lower], r1b.at[db], m1 + 4 + db, to_am)
    lax.fori_loop(4, 12, nearby, 0)

    outs = []

    def enc_chunk(i):
        rows = pl.ds(256 * i, 256)
        ge[rows, :] = lax.dot_general(
            gh[rows, :], proj[...], (((1,), (1,)), ((), ())), preferred_element_type=F32
        )
        if i > 0:
            out_chunk(i - 1)

    def out_chunk(i):
        rows = pl.ds(256 * i, 256)
        copy = pltpu.make_async_copy(ge.at[rows], ge_out.at[rows], ls.at[1 + i])
        copy.start()
        outs.append(copy)

    landed(p1a, pm1)
    landed(p1b, pm1 + 1)
    half = ABLK // 2
    up = pf[ablk(ap), :]
    ps2p[0:half, :] = (up[0:half] + p1a[...].astype(F32)).astype(BF16)
    ps2p[half:, :] = up[half:].astype(BF16)
    down = pf[ablk(am), :]
    ps2m[0:half, :] = down[0:half].astype(BF16)
    ps2m[half:, :] = (down[half:] + p1b[...].astype(F32)).astype(BF16)
    m2 = take(8)
    pm2 = take(2)
    for db in range(4):
        landed(r1a.at[db], m1 + db)
        landed(r1b.at[db], m1 + 4 + db)
        s2p[db, 0:384, :] = (cf[db, 0:384, :] + r1a[db].astype(F32)).astype(BF16)
        s2p[db, 384:768, :] = cf[db, 384:768, :].astype(BF16)
        s2m[db, 0:384, :] = cf[8 + db, 0:384, :].astype(BF16)
        s2m[db, 384:768, :] = (cf[8 + db, 384:768, :] + r1b[db].astype(F32)).astype(BF16)
        if db == 0:
            send(ps2p, pr2p, pm2, to_ap)
            send(ps2m, pr2m, pm2 + 1, to_am)
        else:
            send(s2p.at[db - 1], r2p.at[db - 1], m2 + db - 1, to_ap)
            send(s2m.at[db - 1], r2m.at[db - 1], m2 + 4 + db - 1, to_am)
    enc_chunk(0)
    send(s2p.at[3], r2p.at[3], m2 + 3, to_ap)
    send(s2m.at[3], r2m.at[3], m2 + 7, to_am)
    landed(pr2p, pm2)
    landed(pr2m, pm2 + 1)
    mine = ablk(pa)
    pf[mine, :] = pf[mine, :] + pr2p[...].astype(F32) + pr2m[...].astype(F32)

    def piece(b):
        return pl.ds(pl.multiple_of(pa * ABLK + b * PIECE, 16), PIECE)

    pb0[...] = pf[piece(b2), :].astype(BF16)
    n1 = take(2)
    pn1 = take(2)
    n2 = take(2)
    pn2 = take(2)
    cut = 80

    def finish_a(db):
        landed(r2p.at[db], m2 + db)
        landed(r2m.at[db], m2 + 4 + db)
        return cf[4 + db] + r2p[db].astype(F32) + r2m[db].astype(F32)

    db0[...] = finish_a(0).astype(BF16)
    send(pb0.at[pl.ds(0, cut)], q1a, pn1, to_bp)
    send(pb0.at[pl.ds(cut, PIECE - cut)], q1b, pn1 + 1, to_bm)
    cf[5] = finish_a(1)
    send(db0.at[upper], t1a, n1, to_bp)
    send(db0.at[lower], t1b, n1 + 1, to_bm)
    cf[6] = finish_a(2)
    cf[7] = finish_a(3)
    landed(q1a, pn1)
    landed(q1b, pn1 + 1)
    up = pf[piece(bp), :]
    qs2p[0:cut, :] = (up[0:cut] + q1a[...].astype(F32)).astype(BF16)
    qs2p[cut:, :] = up[cut:].astype(BF16)
    down = pf[piece(bm), :]
    qs2m[0:cut, :] = down[0:cut].astype(BF16)
    qs2m[cut:, :] = (down[cut:] + q1b[...].astype(F32)).astype(BF16)
    landed(t1a, n1)
    landed(t1b, n1 + 1)
    u2p[0:384, :] = (cf[5, 0:384, :] + t1a[...].astype(F32)).astype(BF16)
    u2p[384:768, :] = cf[5, 384:768, :].astype(BF16)
    send(qs2p, qr2p, pn2, to_bp)
    send(qs2m, qr2m, pn2 + 1, to_bm)
    u2m[0:384, :] = cf[7, 0:384, :].astype(BF16)
    u2m[384:768, :] = (cf[7, 384:768, :] + t1b[...].astype(F32)).astype(BF16)
    enc_chunk(1)
    send(u2p, v2p, n2, to_bp)
    send(u2m, v2m, n2 + 1, to_bm)
    landed(qr2p, pn2)
    landed(qr2m, pn2 + 1)
    value = pf[piece(pb), :] + qr2p[...].astype(F32) + qr2m[...].astype(F32)
    ez[...] = value.astype(BF16)
    zp[z] = value.astype(BF16)
    pz = take(NZ)
    landed(v2p, n2)
    landed(v2m, n2 + 1)
    for dz in (4, 3, 5, 2, 6, 1, 7):
        send(ez, zp.at[z], pz + dz, to_z[dz])
    value = cf[6] + v2p[...].astype(F32) + v2m[...].astype(F32)
    value = value.reshape(NZ, D // NZ, LB)
    ef[...] = value
    zs[...] = value.astype(BF16)
    hz = take(NZ)
    enc_chunk(2)
    for dz in (4, 3, 5, 2, 6, 1, 7):
        send(zs.at[(z + dz) % NZ], zr.at[dz], hz + dz, to_z[dz])
    for dz in range(1, NZ):
        landed(zp.at[(z + NZ - dz) % NZ], pz + dz)
    total = zp[0].astype(F32)
    for i in range(1, NZ):
        total = total + zp[i].astype(F32)

    def spot(a, b):
        return pl.ds(pl.multiple_of((core * 4 + a) * ABLK + b * PIECE, 16), PIECE)

    def part(a, b, start, size):
        return pl.ds(pl.multiple_of((core * 4 + a) * ABLK + b * PIECE + start, 16), size)

    po[spot(pa, pb), :] = total.astype(BF16)
    g1 = take(4)
    enc_chunk(3)
    send(po.at[spot(pa, pb)], po.at[spot(pa, pb)], g1, to_bp)
    send(po.at[spot(pa, pb)], po.at[spot(pa, pb)], g1 + 1, to_bm)
    out_chunk(3)
    for dz in range(1, NZ):
        landed(zr.at[dz], hz + dz)
    value = ef[z]
    for dz in range(1, NZ):
        value = value + zr[dz].astype(F32)
    gh_out[...] = value
    landed(po.at[spot(pa, bm)], g1)
    send(po.at[part(pa, bm, 0, cut)], po.at[part(pa, bm, 0, cut)], g1 + 2, to_bp)
    landed(po.at[spot(pa, bp)], g1 + 1)
    send(po.at[part(pa, bp, cut, PIECE - cut)], po.at[part(pa, bp, cut, PIECE - cut)], g1 + 3, to_bm)
    landed(po.at[part(pa, b2, 0, cut)], g1 + 2)
    landed(po.at[part(pa, b2, cut, PIECE - cut)], g1 + 3)

    def wide(a, start, size):
        return pl.ds(pl.multiple_of((core * 4 + a) * ABLK + start, 16), size)

    g2 = take(4)
    g3 = take(4)
    row = po.at[wide(pa, 0, ABLK)]
    send(row, row, g2, to_ap)
    send(row, row, g2 + 1, to_am)
    send(row, row, g3, sib)
    row = po.at[wide(am, 0, ABLK)]
    landed(row, g2)
    send(po.at[wide(am, 0, half)], po.at[wide(am, 0, half)], g2 + 2, to_ap)
    send(row, row, g3 + 1, sib)
    row = po.at[wide(ap, 0, ABLK)]
    landed(row, g2 + 1)
    send(po.at[wide(ap, half, half)], po.at[wide(ap, half, half)], g2 + 3, to_am)
    send(row, row, g3 + 2, sib)
    row = po.at[wide(a2, 0, ABLK)]
    landed(po.at[wide(a2, 0, half)], g2 + 2)
    landed(po.at[wide(a2, half, half)], g2 + 3)
    send(row, row, g3 + 3, sib)
    for i in range(4):
        landed(row, g3 + i)
    last = pltpu.make_async_copy(po, gp_out, ls.at[5])
    last.start()
    for copy in sent:
        copy.wait_send()

    def drain(i, carry):
        across(i).wait_send()
        return carry

    lax.fori_loop(0, 16, drain, 0)
    for copy in outs:
        copy.wait()
    last.wait()
    assert count[0] <= MESSAGES, count[0]


MESSAGES = 128


def scratch():
    v = pltpu.VMEM
    return [
        v((32, SHARD, LB), BF16), v((NBLK, SB, D), BF16), v((NBLK, D, SB), BF16),
        v((D, ROWS), BF16), v((BEAM * LB, D), BF16), v((32, SB, LB), BF16),
        v((ROWS, D), BF16), v((ROWS, D), F32),
        v((16, D, LB), BF16), v((16, D, LB), BF16), v((4, D, LB), BF16), v((12, D, LB), F32),
        v((4, D // 2, LB), BF16), v((4, D // 2, LB), BF16),
        v((4, D, LB), BF16), v((4, D, LB), BF16), v((4, D, LB), BF16), v((4, D, LB), BF16),
        v((D, LB), BF16), v((D // 2, LB), BF16), v((D // 2, LB), BF16),
        v((D, LB), BF16), v((D, LB), BF16), v((D, LB), BF16), v((D, LB), BF16),
        v((NZ, D // NZ, LB), F32), v((NZ, D // NZ, LB), BF16), v((NZ, D // NZ, LB), BF16),
        v((CORE, LB), BF16), v((CORE, LB), BF16), v((CORE, LB), F32),
        v((ABLK, LB), BF16), v((ABLK // 2, LB), BF16), v((ABLK // 2, LB), BF16),
        v((ABLK, LB), BF16), v((ABLK, LB), BF16), v((ABLK, LB), BF16), v((ABLK, LB), BF16),
        v((PIECE, LB), BF16), v((80, LB), BF16), v((PIECE - 80, LB), BF16),
        v((PIECE, LB), BF16), v((PIECE, LB), BF16), v((PIECE, LB), BF16), v((PIECE, LB), BF16),
        v((PIECE, LB), BF16), v((NZ, PIECE, LB), BF16), v((2 * CORE, LB), BF16),
        pltpu.SemaphoreType.DMA((MESSAGES,)), pltpu.SemaphoreType.DMA((MESSAGES,)),
        pltpu.SemaphoreType.DMA((8,)),
    ]


def shards(enc, proj, head_weight, shortlist, positives, weight_num, weight_den):
    size = head_weight.shape[0]
    flat = shortlist.reshape(-1)
    pairs = flat.shape[0]
    match = flat[None, :] == jnp.arange(32, dtype=jnp.int32)[:, None]
    order = jnp.arange(pairs, dtype=jnp.int32)[None, :]
    total = jnp.sum(match.astype(jnp.int32), axis=1)
    one = jnp.min(jnp.where(match, order, pairs - 1), axis=1)
    two = jnp.max(jnp.where(match, order, 0), axis=1)
    tab = jnp.stack([one, one // BEAM, two, two // BEAM])
    live = jnp.stack([total > 0, total > 1]).astype(F32)
    tail = jnp.zeros((16, LB), BF16)
    tail = tail.at[0].set(weight_num.astype(BF16)).at[1].set(weight_den.astype(BF16))
    tail = tail.at[2:].set(1)
    shard = jnp.concatenate(
        [head_weight.reshape(size, D // LB, LB).transpose(1, 0, 2).reshape(D, LB), tail], axis=0
    )
    smem = pl.BlockSpec(memory_space=pltpu.SMEM)
    vmem = pl.BlockSpec(memory_space=pltpu.VMEM)
    anyspace = pl.BlockSpec(memory_space=pl.ANY)
    grad_enc, grad_proj, grad_head = pl.pallas_call(
        kernel,
        out_shape=(
            jax.ShapeDtypeStruct((ROWS, D), F32),
            jax.ShapeDtypeStruct((2 * CORE, LB), BF16),
            jax.ShapeDtypeStruct((D // NZ, LB), F32),
        ),
        in_specs=[smem, smem, smem, vmem, vmem, vmem, vmem],
        out_specs=(anyspace, anyspace, vmem),
        scratch_shapes=scratch(),
        compiler_params=pltpu.CompilerParams(
            collective_id=0, has_side_effects=True, vmem_limit_bytes=62 << 20
        ),
    )(flat, tab, live, enc, proj, shard, positives.reshape(NBLK, SB, -1))
    grad_proj = grad_proj.reshape(D // LB, D, LB).transpose(1, 0, 2).reshape(D, D).astype(F32)
    return (grad_enc, grad_proj, grad_head.T)


def solution(mesh):
    placed = (
        P(("dp", "label"), None),
        P(),
        P("label", None),
        P(("dp", "label"), None),
        P(("dp", "label"), None),
        P("label"),
        P("label"),
    )
    return jax.shard_map(
        shards,
        mesh=mesh,
        in_specs=placed,
        out_specs=(P(("dp", "label"), None), P(), P("label", "dp")),
        check_vma=False,
    )
```

time: 538 us -> 118 us (0.22)
  waiting for transfers between devices: 425 us -> 0 us
  Pallas kernels: 0 us -> 102 us
  matrix products: 33.1 us -> 0 us
  blocking collectives: 23.2 us -> 0 us
  local copies, waits for them, and re-layouts: 32.3 us -> 11.9 us
  between operations: 13.9 us -> 0.68 us
    psum x1 -> x0, waiting for transfers between devices: 262 us -> none  [shards(): lax.psum(lax.dot_general(enc, grad_hidden, (((0,), (0,)), ((), ())), pref...]
    pallas_call x0 -> x1, Pallas kernels: none -> 102 us  [shards(): pl.pallas_call(kernel, out_shape=(jax.ShapeDtypeStruct((ROWS, D), F32), j...]
    reduce_scatter x1 -> x0, waiting for transfers between devices: 98.6 us -> none  [shards(): lax.psum_scatter(grad_all, 'label', scatter_dimension=0, tiled=False)]
    unnamed x5 -> x0, waiting for transfers between devices: 33.4 us -> none
    dot_general x7 -> x0, matrix products: 33.1 us -> none  [the longest x1 9.95 us: shards(): jnp.einsum('cp,pld->cld', chosen, grad_pair, preferred_element_type=jnp.f...]
    all_gather x1 -> x0, waiting for transfers between devices: 30.8 us -> none  [shards(): weights = lax.all_gather(head_weight, 'label')]
    all_gather x1 -> x0, blocking collectives: 23.2 us -> none  [shards(): scales = lax.all_gather(scale, 'label')]
    dot_general x1 -> x0, local copies, waits for them, and re-layouts: 16.6 us -> none  [shards(): jnp.einsum('cp,pld->cld', chosen, grad_pair, preferred_element_type=jnp.f...]
  transfers between devices with their start and end apart: 4 -> 0, of which waited for: 4 -> 0; matrix products, arithmetic and copies ran while one was open for 5% -> 0% of each run, Pallas kernels for 0% -> 0%
where the time goes in v2:
time: 118 us
  Pallas kernels  102 us (86%)
  local copies, waits for them, and re-layouts  11.9 us (10%)
  other arithmetic  3.36 us (3%)
    pallas_call x1, Pallas kernels, shards(): pl.pallas_call(kernel, out_shape=(jax.ShapeDtypeStruct((ROWS, D), F32), j...  102 us
    unnamed x10, local copies, waits for them, and re-layouts  9.94 us

profile of v2, /device:TPU:1, one launch (start us, length us, event | category | flops | bytes accessed | tf_op | source)
XLA Modules:
  0.0 118.2 jit_solution(6988340467515274931)
XLA Ops:
  0.6 0.7 convert_bitcast_fusion.1
  1.3 0.7 convert_bitcast_fusion
  2.0 0.8 copy.20
  2.7 0.1 reshape.215.sl
  2.8 0.0 copy-start.1
  2.8 0.2 convert_reduce_fusion
  3.0 0.6 add_convert_fusion.live
  3.6 0.6 pad_add_fusion.tab
  4.2 0.1 scatter.14
  4.3 1.1 copy.21
  5.3 0.2 copy.22
  5.5 0.7 pad_maximum_fusion.shard
  6.2 1.8 %copy.23 = s32[1024,8]{1,0:T(8,128)} copy(s32[1024,8]{0,1:T(8,128)} %param.17) | data formatting | bytes 65536 | tf_op args[4]
  8.0 0.0 copy-done.1
  8.0 102.3 %shard_map.94 = (f32[1024,768]{1,0:T(8,128)}, bf16[4608,128]{1,0:T(8,128)(2,1)}, f32[96,128]{1,0:T(8,128)}) custom-call(s32[32]{0:T(128)} %copy-done.1, s32[4,32]{1,0:T(4,128)} %pad_add_fusion.tab, f32[2,32]{1,0:T(2,128)} %add_convert_fusion.live, bf16[1024,768]{1,0:T(8,128)(2,1)} %enc.1, bf16[768,768]{1,0:T(8,128)(2,1)} %proj.1, ...), custom_call_target="tpu_custom_call" | custom-call | tf_op jit(solution)/shard_map/pallas_call | solution.py:485
  110.2 1.6 %copy.24 = f32[6,768,128]{1,2,0:T(8,128)S(1)} copy(bf16[6,768,128]{2,1,0:T(8,128)(2,1)} %bitcast.25) | data formatting | bytes 3538944 | tf_op jit(solution)/shard_map/convert_element_type | solution.py:499
  111.8 2.0 %copy.25 = f32[768,768]{1,0:T(8,128)} copy(f32[768,768]{0,1:T(8,128)S(1)} %bitcast.23) | data formatting | bytes 4718592
  113.8 0.0 copy-start
  113.8 3.8 %copy.30 = f32[1024,768]{1,0:T(8,128)} copy(f32[1024,768]{1,0:T(8,128)} %get-tuple-element.61) | data formatting | bytes 6291456
  117.5 0.0 copy-done
  117.5 0.6 copy.31
  (5 shorter events, 0.1 us)
Async XLA Ops:
  2.8 5.2 %copy-start.1 = (s32[32]{0:T(128)}, s32[32]{0:T(128)S(1)}, u32[]{:S(2)}) copy-start(s32[32]{0:T(128)S(1)} %reshape.215.sl) | copy-start | bytes 388
  113.8 3.8 %copy-start = (f32[96,128]{1,0:T(8,128)S(1)}, f32[96,128]{1,0:T(8,128)}, u32[]{:S(2)}) copy-start(f32[96,128]{1,0:T(8,128)} %get-tuple-element.44) | copy-start | bytes 147460

commit v3 on v1

v3 whole, which is shorter than its diff:
```python
import jax
import jax.numpy as jnp
from jax import lax
from jax.experimental import pallas as pl
from jax.experimental.pallas import tpu as pltpu
from jax.sharding import PartitionSpec as P

MESH = pl.DeviceIdType.MESH
F32 = jnp.float32
BF16 = jnp.bfloat16

D = 768
LB = 128
SB = 128
BEAM = 4
NBLK = 8
ROWS = NBLK * SB
SHARD = D + 16
HALF0, HALF1 = 400, 384
NZ = 8
PIECE = 144
ABLK = 4 * PIECE
CORE = 4 * ABLK


def lid(pa, pb, core):
    xx = pa + core * (pb - pa)
    yy = pb + core * (pa - pb)
    return (yy * 4 + xx) * 2 + core


def kernel(
    sl, tab, num, den, post, enc_in, proj_in, head_in,
    ge_out, gp_out, gh_out,
    enc, proj, wl, pos, hid, hidt, enct, w4, gl, gh, ge,
    sb, rb, cb, cf, ra, dbs, rbb, ef, zs, zr,
    ps0, pr0, pf, pas, pra, pbs, prb, ez, zp, po,
    ss, rs, ls,
):
    z = lax.axis_index("dp")
    me = lax.axis_index("label")
    core = me % 2
    x = (me // 2) % 4
    y = me // 8
    pa = x + core * (y - x)
    pb = y + core * (x - y)
    other = 1 - core
    ap, am, a2 = (pa + 1) % 4, (pa + 3) % 4, (pa + 2) % 4
    bp, bm, b2 = (pb + 1) % 4, (pb + 3) % 4, (pb + 2) % 4
    sib = {"label": me + 1 - 2 * core}
    to_ap = {"label": lid(ap, pb, core)}
    to_am = {"label": lid(am, pb, core)}
    to_a2 = {"label": lid(a2, pb, core)}
    to_bp = {"label": lid(pa, bp, core)}
    to_bm = {"label": lid(pa, bm, core)}
    to_b2 = {"label": lid(pa, b2, core)}
    to_z = [None] + [{"dp": (z + dz) % NZ} for dz in range(1, NZ)]

    barrier = pltpu.get_barrier_semaphore()
    greeted = [sib, to_ap, to_am, to_a2, to_bp, to_bm, to_b2] + to_z[1:]
    for device in greeted:
        pl.semaphore_signal(barrier, inc=1, device_id=device, device_id_type=MESH)

    loads = []
    for j in range(D // LB):
        loads.append(pltpu.make_async_copy(
            head_in.at[:, pl.ds(j * LB, LB)], wl.at[me, pl.ds(j * LB, LB)], ls.at[j]))
    loads.append(pltpu.make_async_copy(proj_in, proj, ls.at[6]))
    loads.append(pltpu.make_async_copy(enc_in, enc, ls.at[7]))
    for load in loads:
        load.start()
    line = lax.broadcasted_iota(jnp.int32, (16, LB), 0)
    tail = jnp.where(line == 0, num[...], jnp.where(line == 1, den[...], 1))
    wl[me, D:SHARD, :] = tail.astype(F32).astype(BF16)

    count = [0]
    sent = []

    def take(n=1):
        first = count[0]
        count[0] += n
        return first

    def remote(src, dst, i, device):
        return pltpu.make_async_remote_copy(
            src_ref=src, dst_ref=dst, send_sem=ss.at[i], recv_sem=rs.at[i],
            device_id=device, device_id_type=MESH,
        )

    def send(src, dst, i, device):
        copy = remote(src, dst, i, device)
        copy.start()
        sent.append(copy)

    def landed(dst, i):
        remote(dst, dst, i, sib).wait_recv()

    def hidden_chunk(i):
        for b in (2 * i, 2 * i + 1):
            pos[b] = post[:, b * SB:(b + 1) * SB].T
        rows = enc[pl.ds(256 * i, 256), :]
        value = jnp.dot(rows, proj[...], preferred_element_type=F32).astype(BF16)
        hid[2 * i] = value[:SB]
        hid[2 * i + 1] = value[SB:]
        hidt[2 * i] = value[:SB].T
        hidt[2 * i + 1] = value[SB:].T
        enct[:, pl.ds(256 * i, 256)] = rows.T

    for load in loads[:6]:
        load.wait()
    pl.semaphore_wait(barrier, len(greeted))
    top, bottom = pl.ds(0, HALF0), pl.ds(HALF0, HALF1)
    first = take(3)
    base = take(16)
    near = take(16)

    def slot(a, b):
        return wl.at[lid(a, b, core)]

    columns = [pa, am, ap, a2]
    own = wl.at[me]
    early = [remote(own, own, first, to_ap), remote(own, own, first + 1, to_am)]
    for copy in early:
        copy.start()
    send(own, own, first + 2, to_a2)
    send(own, own, near, sib)
    for copy in early:
        copy.wait_send()
    send(own, own, base, to_bp)
    send(own, own, base + 1, to_bm)
    loads[6].wait()
    loads[7].wait()
    hidden_chunk(0)

    def spread(j):
        held = slot(columns[j], pb)
        send(held, held, base + 4 * j, to_bp)
        send(held, held, base + 4 * j + 1, to_bm)
        send(held, held, near + j, sib)

    def forward(j):
        a = columns[j]
        held = slot(a, bm)
        landed(held, base + 4 * j)
        send(held.at[top], held.at[top], base + 4 * j + 2, to_bp)
        send(held, held, near + 4 + j, sib)
        held = slot(a, bp)
        landed(held, base + 4 * j + 1)
        send(held.at[bottom], held.at[bottom], base + 4 * j + 3, to_bm)
        send(held, held, near + 8 + j, sib)

    landed(slot(am, pb), first)
    spread(1)
    landed(slot(ap, pb), first + 1)
    spread(2)
    forward(0)
    landed(slot(a2, pb), first + 2)
    spread(3)
    hidden_chunk(1)
    forward(1)
    hidden_chunk(2)
    forward(2)
    hidden_chunk(3)
    forward(3)
    for j in (0, 1, 2, 3):
        held = slot(columns[j], b2)
        landed(held.at[top], base + 4 * j + 2)
        landed(held.at[bottom], base + 4 * j + 3)
        send(held, held, near + 12 + j, sib)
    for i in range(16):
        landed(own, near + i)

    place = lax.broadcasted_iota(jnp.int32, (SB, LB), 1)

    def block(b, carry):
        wanted = pos[b]
        for k in range(BEAM):
            c = sl[k, b]
            for j in range(D // LB):
                w4[k * LB:(k + 1) * LB, j * LB:(j + 1) * LB] = wl[c, j * LB:(j + 1) * LB, :]
        rows = hid[b]
        parts = []
        for k in range(BEAM):
            c = sl[k, b]
            ends = wl[c, D:SHARD, :].astype(F32)
            scale = ends[0:1] / ends[1:2]
            logits = lax.dot_general(
                rows, w4[k * LB:(k + 1) * LB, :], (((1,), (1,)), ((), ())),
                preferred_element_type=F32,
            )
            hit = wanted[:, 0:1] == place + k * LB
            for column in range(1, wanted.shape[1]):
                hit = hit | (wanted[:, column:column + 1] == place + k * LB)
            target = jnp.where(hit, 1.0, 0.0)
            part = (scale * (jax.nn.sigmoid(logits) - target) / SB).astype(BF16)
            gl[b * BEAM + k] = part
            parts.append(part)
        total = jnp.dot(jnp.concatenate(parts, axis=1), w4[...], preferred_element_type=F32)
        gh[pl.ds(pl.multiple_of(b * SB, SB), SB), :] = total.astype(BF16)
        return carry

    lax.fori_loop(0, NBLK, block, 0)

    def proj_half(which):
        lanes = pl.ds(pl.multiple_of(which * (D // 2), 128), D // 2)
        return jnp.dot(enct[...], gh[:, lanes], preferred_element_type=F32)

    value = proj_half(other)
    for j in range(3):
        ps0[j * D:(j + 1) * D, :] = value[:, j * LB:(j + 1) * LB].astype(BF16)
    value = proj_half(core)
    pair0 = take()
    send(ps0, pr0, pair0, sib)
    for j in range(3):
        pf[j * D:(j + 1) * D, :] = value[:, j * LB:(j + 1) * LB]

    def cluster(c):
        code = tab[c]
        one = lax.rem(code, 32)
        two = lax.rem(lax.div(code, 32), 32)
        total = lax.div(code, 1024)
        left = jnp.concatenate([hidt[lax.div(one, BEAM)], hidt[lax.div(two, BEAM)]], axis=1)
        up = gl[one].astype(F32) * jnp.minimum(total, 1).astype(F32)
        down = gl[two].astype(F32) * jnp.maximum(total - 1, 0).astype(F32)
        right = jnp.concatenate([up.astype(BF16), down.astype(BF16)], axis=0)
        return jnp.dot(left, right, preferred_element_type=F32)

    cross = take(16)

    def across(i):
        return remote(sb.at[i], rb.at[i], cross + i, sib)

    def for_other(i, carry):
        c = lid((pb + 6 - i % 4) % 4, (pa + 6 - i // 4) % 4, other)
        sb[i] = cluster(c).astype(BF16)

        @pl.when(i > 0)
        def _():
            across(i - 1).start()

        return carry

    lax.fori_loop(0, 16, for_other, 0)

    def ablk(a):
        return pl.ds(pl.multiple_of(a * ABLK, 16), ABLK)

    landed(pr0, pair0)
    across(15).start()
    pm = take(3)

    def pack(r, a):
        pas[r] = (pf[ablk(a), :] + pr0[ablk(a), :].astype(F32)).astype(BF16)

    pack(2, a2)
    pack(0, ap)
    send(pas.at[2], pra.at[2], pm + 2, to_a2)
    pack(1, am)
    send(pas.at[0], pra.at[0], pm, to_ap)
    mine = ablk(pa)
    pf[mine, :] = pf[mine, :] + pr0[mine, :].astype(F32)
    send(pas.at[1], pra.at[1], pm + 1, to_am)

    hm = take(12)

    def along_a(db, r):
        return remote(cb.at[db * 3 + r], ra.at[r, db], hm + db * 3 + r, (to_ap, to_am, to_a2)[r])

    def own_clusters(db, carry):
        def value_of(da):
            c = lid((pa + 6 - da) % 4, (pb + 6 - db) % 4, core)
            value = cluster(c)
            across(db * 4 + da).wait_recv()
            return value + rb[db * 4 + da].astype(F32)

        cb[db * 3 + 2] = value_of(0).astype(BF16)
        cb[db * 3] = value_of(1).astype(BF16)
        along_a(db, 2).start()
        cb[db * 3 + 1] = value_of(3).astype(BF16)
        along_a(db, 0).start()
        cf[db] = value_of(2)
        along_a(db, 1).start()
        return carry

    lax.fori_loop(0, 4, own_clusters, 0)

    outs = []

    def enc_chunk(i):
        rows = pl.ds(256 * i, 256)
        ge[rows, :] = lax.dot_general(
            gh[rows, :], proj[...], (((1,), (1,)), ((), ())), preferred_element_type=F32
        )
        if i > 0:
            out_chunk(i - 1)

    def out_chunk(i):
        rows = pl.ds(256 * i, 256)
        copy = pltpu.make_async_copy(ge.at[rows], ge_out.at[rows], ls.at[8 + i])
        copy.start()
        outs.append(copy)

    enc_chunk(0)
    for r in range(3):
        landed(pra.at[r], pm + r)
    value = pf[mine, :] + pra[0].astype(F32) + pra[1].astype(F32) + pra[2].astype(F32)
    pf[mine, :] = value
    pbs[...] = value.astype(BF16)

    def piece(b):
        return pl.ds(pl.multiple_of(b * PIECE, 16), PIECE)

    pn = take(3)
    enc_chunk(1)
    send(pbs.at[piece(b2)], prb.at[2], pn + 2, to_b2)
    send(pbs.at[piece(bp)], prb.at[0], pn, to_bp)
    send(pbs.at[piece(bm)], prb.at[1], pn + 1, to_bm)
    hn = take(3)

    def finish_a(db):
        for r in range(3):
            landed(ra.at[r, db], hm + db * 3 + r)
        return cf[db] + ra[0, db].astype(F32) + ra[1, db].astype(F32) + ra[2, db].astype(F32)

    dbs[2] = finish_a(0).astype(BF16)
    for r in range(3):
        landed(prb.at[r], pn + r)
    spot_rows = pl.ds(pl.multiple_of(pa * ABLK + pb * PIECE, 16), PIECE)
    value = pf[spot_rows, :] + prb[0].astype(F32) + prb[1].astype(F32) + prb[2].astype(F32)
    ez[...] = value.astype(BF16)
    zp[z] = value.astype(BF16)
    pz = take(NZ)
    send(dbs.at[2], rbb.at[2], hn + 2, to_b2)
    enc_chunk(2)
    for dz in (4, 3, 5, 2, 6, 1, 7):
        send(ez, zp.at[z], pz + dz, to_z[dz])
    dbs[0] = finish_a(1).astype(BF16)
    enc_chunk(3)
    send(dbs.at[0], rbb.at[0], hn, to_bp)
    out_chunk(3)
    cf[2] = finish_a(2)
    dbs[1] = finish_a(3).astype(BF16)
    for dz in range(1, NZ):
        landed(zp.at[(z + NZ - dz) % NZ], pz + dz)
    send(dbs.at[1], rbb.at[1], hn + 1, to_bm)
    total = zp[0].astype(F32)
    for i in range(1, NZ):
        total = total + zp[i].astype(F32)

    def spot(a, b):
        return po.at[pl.ds(pl.multiple_of((core * 4 + a) * ABLK + b * PIECE, 16), PIECE)]

    def wide(a):
        return po.at[pl.ds(pl.multiple_of((core * 4 + a) * ABLK, 16), ABLK)]

    po[pl.ds(pl.multiple_of((core * 4 + pa) * ABLK + pb * PIECE, 16), PIECE), :] = total.astype(BF16)
    g1 = take(3)
    landed(rbb.at[2], hn + 2)
    landed(rbb.at[0], hn)
    for r, device in enumerate((to_bp, to_bm, to_b2)):
        send(spot(pa, pb), spot(pa, pb), g1 + r, device)
    landed(rbb.at[1], hn + 1)
    value = cf[2] + rbb[0].astype(F32) + rbb[1].astype(F32) + rbb[2].astype(F32)
    value = value.reshape(NZ, D // NZ, LB)
    ef[...] = value
    zs[...] = value.astype(BF16)
    hz = take(NZ)
    landed(spot(pa, bm), g1)
    for dz in (4, 3, 5, 2, 6, 1, 7):
        send(zs.at[(z + dz) % NZ], zr.at[dz], hz + dz, to_z[dz])
    landed(spot(pa, bp), g1 + 1)
    landed(spot(pa, b2), g1 + 2)
    g2 = take(3)
    g3 = take(4)
    for r, device in enumerate((to_ap, to_am, to_a2)):
        send(wide(pa), wide(pa), g2 + r, device)
    send(wide(pa), wide(pa), g3, sib)
    for r, a in enumerate((am, ap, a2)):
        landed(wide(a), g2 + r)
        send(wide(a), wide(a), g3 + 1 + r, sib)
    for dz in range(1, NZ):
        landed(zr.at[dz], hz + dz)
    value = ef[z]
    for dz in range(1, NZ):
        value = value + zr[dz].astype(F32)
    gh_out[...] = value
    for i in range(4):
        landed(wide(pa), g3 + i)
    for j in range(D // LB):
        copy = pltpu.make_async_copy(
            po.at[pl.ds(j * D, D)], gp_out.at[:, pl.ds(j * LB, LB)], ls.at[j])
        copy.start()
        outs.append(copy)
    for copy in sent:
        copy.wait_send()

    def drain(i, carry):
        across(i).wait_send()
        return carry

    lax.fori_loop(0, 16, drain, 0)

    def drain_a(db, carry):
        for r in range(3):
            along_a(db, r).wait_send()
        return carry

    lax.fori_loop(0, 4, drain_a, 0)
    for copy in outs:
        copy.wait()
    assert count[0] <= MESSAGES, count[0]


MESSAGES = 128


def scratch():
    v = pltpu.VMEM
    return [
        v((ROWS, D), BF16), v((D, D), BF16),
        v((32, SHARD, LB), BF16), v((NBLK, SB, 8), jnp.int32),
        v((NBLK, SB, D), BF16), v((NBLK, D, SB), BF16),
        v((D, ROWS), BF16), v((BEAM * LB, D), BF16), v((32, SB, LB), BF16),
        v((ROWS, D), BF16), v((ROWS, D), F32),
        v((16, D, LB), BF16), v((16, D, LB), BF16), v((12, D, LB), BF16), v((4, D, LB), F32),
        v((3, 4, D, LB), BF16), v((3, D, LB), BF16), v((3, D, LB), BF16),
        v((NZ, D // NZ, LB), F32), v((NZ, D // NZ, LB), BF16), v((NZ, D // NZ, LB), BF16),
        v((CORE, LB), BF16), v((CORE, LB), BF16), v((CORE, LB), F32),
        v((3, ABLK, LB), BF16), v((3, ABLK, LB), BF16),
        v((ABLK, LB), BF16), v((3, PIECE, LB), BF16),
        v((PIECE, LB), BF16), v((NZ, PIECE, LB), BF16), v((2 * CORE, LB), BF16),
        pltpu.SemaphoreType.DMA((MESSAGES,)), pltpu.SemaphoreType.DMA((MESSAGES,)),
        pltpu.SemaphoreType.DMA((12,)),
    ]


def shards(enc, proj, head_weight, shortlist, positives, weight_num, weight_den):
    ids = jnp.arange(32, dtype=jnp.int32)[:, None, None]
    match = shortlist[None] == ids
    order = jnp.arange(NBLK * BEAM, dtype=jnp.int32).reshape(1, NBLK, BEAM)
    total = jnp.sum(match.astype(jnp.int32), axis=(1, 2))
    one = jnp.min(jnp.where(match, order, NBLK * BEAM - 1), axis=(1, 2))
    two = jnp.max(jnp.where(match, order, 0), axis=(1, 2))
    tab = one + 32 * two + 1024 * total
    smem = pl.BlockSpec(memory_space=pltpu.SMEM)
    vmem = pl.BlockSpec(memory_space=pltpu.VMEM)
    anyspace = pl.BlockSpec(memory_space=pl.ANY)
    grad_enc, grad_proj, grad_head = pl.pallas_call(
        kernel,
        out_shape=(
            jax.ShapeDtypeStruct((ROWS, D), F32),
            jax.ShapeDtypeStruct((D, D), BF16),
            jax.ShapeDtypeStruct((D // NZ, LB), F32),
        ),
        in_specs=[smem, smem, vmem, vmem, vmem, anyspace, anyspace, anyspace],
        out_specs=(anyspace, anyspace, vmem),
        scratch_shapes=scratch(),
        compiler_params=pltpu.CompilerParams(
            collective_id=0, has_side_effects=True, vmem_limit_bytes=60 << 20
        ),
    )(
        shortlist.T, tab, weight_num.reshape(1, LB), weight_den.reshape(1, LB), positives.T,
        enc, proj, head_weight,
    )
    return (grad_enc, grad_proj.astype(F32), grad_head.T)


def solution(mesh):
    placed = (
        P(("dp", "label"), None),
        P(),
        P("label", None),
        P(("dp", "label"), None),
        P(("dp", "label"), None),
        P("label"),
        P("label"),
    )
    return jax.shard_map(
        shards,
        mesh=mesh,
        in_specs=placed,
        out_specs=(P(("dp", "label"), None), P(), P("label", "dp")),
        check_vma=False,
    )
```

time: 538 us -> 97.1 us (0.18)
  waiting for transfers between devices: 425 us -> 0 us
  Pallas kernels: 0 us -> 88.9 us
  matrix products: 33.1 us -> 0 us
  local copies, waits for them, and re-layouts: 32.3 us -> 2.29 us
  blocking collectives: 23.2 us -> 0 us
  between operations: 13.9 us -> 0.66 us
    psum x1 -> x0, waiting for transfers between devices: 262 us -> none  [shards(): lax.psum(lax.dot_general(enc, grad_hidden, (((0,), (0,)), ((), ())), pref...]
    reduce_scatter x1 -> x0, waiting for transfers between devices: 98.6 us -> none  [shards(): lax.psum_scatter(grad_all, 'label', scatter_dimension=0, tiled=False)]
    pallas_call x0 -> x1, Pallas kernels: none -> 88.9 us  [shards(): pl.pallas_call(kernel, out_shape=(jax.ShapeDtypeStruct((ROWS, D), F32), j...]
    unnamed x5 -> x0, waiting for transfers between devices: 33.4 us -> none
    dot_general x7 -> x0, matrix products: 33.1 us -> none  [the longest x1 9.95 us: shards(): jnp.einsum('cp,pld->cld', chosen, grad_pair, preferred_element_type=jnp.f...]
    all_gather x1 -> x0, waiting for transfers between devices: 30.8 us -> none  [shards(): weights = lax.all_gather(head_weight, 'label')]
    all_gather x1 -> x0, blocking collectives: 23.2 us -> none  [shards(): scales = lax.all_gather(scale, 'label')]
    dot_general x1 -> x0, local copies, waits for them, and re-layouts: 16.6 us -> none  [shards(): jnp.einsum('cp,pld->cld', chosen, grad_pair, preferred_element_type=jnp.f...]
  transfers between devices with their start and end apart: 4 -> 0, of which waited for: 4 -> 0; matrix products, arithmetic and copies ran while one was open for 5% -> 0% of each run, Pallas kernels for 0% -> 0%
where the time goes in v3:
time: 97.1 us; the launch traced here: 96.2 us
  Pallas kernels  88.9 us (92%)
  other arithmetic  4.29 us (4%)
  local copies, waits for them, and re-layouts  2.29 us (2%)
    pallas_call x1, Pallas kernels, shards(): pl.pallas_call(kernel, out_shape=(jax.ShapeDtypeStruct((ROWS, D), F32), j...  88.9 us
    convert_element_type x1, other arithmetic, shards(): return (grad_enc, grad_proj.astype(F32), grad_head.T)  3 us
    unnamed x6, local copies, waits for them, and re-layouts  2.29 us

profile of v3, /device:TPU:1, one launch (start us, length us, event | category | flops | bytes accessed | tf_op | source)
XLA Modules:
  0.0 96.2 jit_solution(12977343042891359473)
XLA Ops:
  0.6 0.8 select_reduce_fusion
  1.4 0.5 multiply_add_fusion.1.tab
  1.9 88.9 %shard_map.94 = (f32[1024,768]{1,0:T(8,128)}, bf16[768,768]{1,0:T(8,128)(2,1)}, f32[96,128]{1,0:T(8,128)}) custom-call(s32[4,8]{1,0:T(4,128)} %bitcast.7, s32[32]{0:T(128)} %multiply_add_fusion.1.tab, s32[1,128]{1,0:T(1,128)} %bitcast.8, s32[1,128]{1,0:T(1,128)} %bitcast.9, s32[8,1024]{1,0:T(8,128)} %bitcast.6, bf16[1024,768]{1,0:T(8,128)(2,1)} %enc_in.1, ...), custom_call_target="tpu_custom_call" | custom-call | tf_op jit(solution)/shard_map/pallas_call | solution.py:448
  90.9 0.0 copy-start
  90.9 3.0 %convert_element_type.7 = f32[768,768]{1,0:T(8,128)} convert(bf16[768,768]{1,0:T(8,128)(2,1)} %get-tuple-element.7) | non-fusion elementwise | flops 589824 | bytes 3538944 | tf_op jit(solution)/shard_map/convert_element_type | solution.py:465
  93.9 0.0 copy-done
  93.9 0.0 copy-start.1
  93.9 1.7 %copy.13 = f32[1024,768]{1,0:T(8,128)} copy(f32[1024,768]{1,0:T(8,128)S(1)} %copy-done) | data formatting | bytes 6291456
  95.6 0.0 copy-done.1
  95.6 0.6 copy.14
  (1 shorter events, 0.0 us)
Async XLA Ops:
  90.9 3.0 %copy-start = (f32[1024,768]{1,0:T(8,128)S(1)}, f32[1024,768]{1,0:T(8,128)}, u32[]{:S(2)}) copy-start(f32[1024,768]{1,0:T(8,128)} %get-tuple-element.15) | copy-start | bytes 9437188
  93.9 1.7 %copy-start.1 = (f32[96,128]{1,0:T(8,128)S(1)}, f32[96,128]{1,0:T(8,128)}, u32[]{:S(2)}) copy-start(f32[96,128]{1,0:T(8,128)} %get-tuple-element.8) | copy-start | bytes 147460

commit v4 on v3

--- a/solution.py
+++ b/solution.py
@@ -30,11 +30,11 @@
 
 
 def kernel(
-    sl, tab, num, den, post, enc_in, proj_in, head_in,
-    ge_out, gp_out, gh_out,
-    enc, proj, wl, pos, hid, hidt, enct, w4, gl, gh, ge,
-    sb, rb, cb, cf, ra, dbs, rbb, ef, zs, zr,
-    ps0, pr0, pf, pas, pra, pbs, prb, ez, zp, po,
+    sl, tab, num_in, den_in, post_in, enc_in, proj_in, head_in,
+    ge, gp_out, gh_out,
+    num, den, post, enc, proj, wl, pos, hid, hidt, hidt_s, enct, enct_s, w4, gl, gl_s, gh, gh_s,
+    cb, cf, ra, dbs, rbb, ef, zs, zr,
+    pf, pas, pra, pbs, prb, ez, zp, po, tab_s,
     ss, rs, ls,
 ):
     z = lax.axis_index("dp")
@@ -67,8 +67,15 @@
             head_in.at[:, pl.ds(j * LB, LB)], wl.at[me, pl.ds(j * LB, LB)], ls.at[j]))
     loads.append(pltpu.make_async_copy(proj_in, proj, ls.at[6]))
     loads.append(pltpu.make_async_copy(enc_in, enc, ls.at[7]))
-    for load in loads:
+    small = [
+        pltpu.make_async_copy(num_in, num, ls.at[8]),
+        pltpu.make_async_copy(den_in, den, ls.at[9]),
+    ]
+    loads.append(pltpu.make_async_copy(post_in, post, ls.at[10]))
+    for load in small + loads:
         load.start()
+    for load in small:
+        load.wait()
     line = lax.broadcasted_iota(jnp.int32, (16, LB), 0)
     tail = jnp.where(line == 0, num[...], jnp.where(line == 1, den[...], 1))
     wl[me, D:SHARD, :] = tail.astype(F32).astype(BF16)
@@ -104,7 +111,14 @@
         hid[2 * i + 1] = value[SB:]
         hidt[2 * i] = value[:SB].T
         hidt[2 * i + 1] = value[SB:].T
-        enct[:, pl.ds(256 * i, 256)] = rows.T
+        enct[i] = rows.T
+
+    share = take(8)
+
+    def share_chunk(i):
+        pair = pl.ds(2 * i, 2)
+        send(hidt.at[pair], hidt_s.at[pair], share + 2 * i, sib)
+        send(enct.at[i], enct_s.at[i], share + 2 * i + 1, sib)
 
     for load in loads[:6]:
         load.wait()
@@ -128,8 +142,11 @@
         copy.wait_send()
     send(own, own, base, to_bp)
     send(own, own, base + 1, to_bm)
+    tabled = take()
+    send(tab, tab_s, tabled, sib)
     loads[6].wait()
     loads[7].wait()
+    loads[8].wait()
     hidden_chunk(0)
 
     def spread(j):
@@ -156,12 +173,16 @@
     forward(0)
     landed(slot(a2, pb), first + 2)
     spread(3)
+    share_chunk(0)
     hidden_chunk(1)
     forward(1)
+    share_chunk(1)
     hidden_chunk(2)
     forward(2)
+    share_chunk(2)
     hidden_chunk(3)
     forward(3)
+    share_chunk(3)
     for j in (0, 1, 2, 3):
         held = slot(columns[j], b2)
         landed(held.at[top], base + 4 * j + 2)
@@ -171,6 +192,16 @@
         landed(own, near + i)
 
     place = lax.broadcasted_iota(jnp.int32, (SB, LB), 1)
+
+    lent = take(16)
+
+    def lend_gl(b):
+        rows = pl.ds(pl.multiple_of(b * BEAM, BEAM), BEAM)
+        return remote(gl.at[rows], gl_s.at[rows], lent + b, sib)
+
+    def lend_gh(b):
+        rows = pl.ds(pl.multiple_of(b * SB, SB), SB)
+        return remote(gh.at[rows], gh_s.at[rows], lent + 8 + b, sib)
 
     def block(b, carry):
         wanted = pos[b]
@@ -195,83 +226,90 @@
             part = (scale * (jax.nn.sigmoid(logits) - target) / SB).astype(BF16)
             gl[b * BEAM + k] = part
             parts.append(part)
+
+        @pl.when(b > 0)
+        def _():
+            lend_gl(b - 1).start()
+            lend_gh(b - 1).start()
+
         total = jnp.dot(jnp.concatenate(parts, axis=1), w4[...], preferred_element_type=F32)
         gh[pl.ds(pl.multiple_of(b * SB, SB), SB), :] = total.astype(BF16)
         return carry
 
     lax.fori_loop(0, NBLK, block, 0)
 
-    def proj_half(which):
-        lanes = pl.ds(pl.multiple_of(which * (D // 2), 128), D // 2)
-        return jnp.dot(enct[...], gh[:, lanes], preferred_element_type=F32)
-
-    value = proj_half(other)
+    lend_gl(NBLK - 1).start()
+
+    def proj_part(left, right, j, n):
+        lanes = pl.ds(pl.multiple_of(core * (D // 2) + j * LB, 128), n * LB)
+        whole = jnp.concatenate([left[i] for i in range(4)], axis=1)
+        return jnp.dot(whole, right[:, lanes], preferred_element_type=F32)
+
+    value = proj_part(enct, gh, 0, 1)
+    lend_gh(NBLK - 1).start()
+    pf[0:D, :] = value
+    value = proj_part(enct, gh, 1, 2)
+    pf[D:2 * D, :] = value[:, :LB]
+    pf[2 * D:3 * D, :] = value[:, LB:]
+    for i in range(4):
+        landed(enct_s.at[i], share + 2 * i + 1)
+
+    def arrive_gh(b, carry):
+        lend_gh(b).wait_recv()
+        return carry
+
+    lax.fori_loop(0, NBLK, arrive_gh, 0)
+    value = proj_part(enct_s, gh_s, 0, 3)
     for j in range(3):
-        ps0[j * D:(j + 1) * D, :] = value[:, j * LB:(j + 1) * LB].astype(BF16)
-    value = proj_half(core)
-    pair0 = take()
-    send(ps0, pr0, pair0, sib)
-    for j in range(3):
-        pf[j * D:(j + 1) * D, :] = value[:, j * LB:(j + 1) * LB]
-
-    def cluster(c):
-        code = tab[c]
+        rows = slice(j * D, (j + 1) * D)
+        pf[rows, :] = pf[rows, :] + value[:, j * LB:(j + 1) * LB]
+
+    def ablk(a):
+        return pl.ds(pl.multiple_of(a * ABLK, 16), ABLK)
+
+    pm = take(3)
+    mine = ablk(pa)
+    pas[2] = pf[ablk(a2), :].astype(BF16)
+    pas[0] = pf[ablk(ap), :].astype(BF16)
+    pas[1] = pf[ablk(am), :].astype(BF16)
+    for i in range(4):
+        landed(hidt_s.at[pl.ds(2 * i, 2)], share + 2 * i)
+    landed(tab_s, tabled)
+
+    def arrive_gl(b, carry):
+        lend_gl(b).wait_recv()
+        return carry
+
+    lax.fori_loop(0, NBLK, arrive_gl, 0)
+    send(pas.at[2], pra.at[2], pm + 2, to_a2)
+    send(pas.at[0], pra.at[0], pm, to_ap)
+    send(pas.at[1], pra.at[1], pm + 1, to_am)
+
+    hm = take(12)
+
+    def along_a(db, r):
+        return remote(cb.at[db * 3 + r], ra.at[r, db], hm + db * 3 + r, (to_ap, to_am, to_a2)[r])
+
+    def halves(c, table, turned, grads):
+        code = table[0, c]
         one = lax.rem(code, 32)
         two = lax.rem(lax.div(code, 32), 32)
         total = lax.div(code, 1024)
-        left = jnp.concatenate([hidt[lax.div(one, BEAM)], hidt[lax.div(two, BEAM)]], axis=1)
-        up = gl[one].astype(F32) * jnp.minimum(total, 1).astype(F32)
-        down = gl[two].astype(F32) * jnp.maximum(total - 1, 0).astype(F32)
-        right = jnp.concatenate([up.astype(BF16), down.astype(BF16)], axis=0)
-        return jnp.dot(left, right, preferred_element_type=F32)
-
-    cross = take(16)
-
-    def across(i):
-        return remote(sb.at[i], rb.at[i], cross + i, sib)
-
-    def for_other(i, carry):
-        c = lid((pb + 6 - i % 4) % 4, (pa + 6 - i // 4) % 4, other)
-        sb[i] = cluster(c).astype(BF16)
-
-        @pl.when(i > 0)
-        def _():
-            across(i - 1).start()
-
-        return carry
-
-    lax.fori_loop(0, 16, for_other, 0)
-
-    def ablk(a):
-        return pl.ds(pl.multiple_of(a * ABLK, 16), ABLK)
-
-    landed(pr0, pair0)
-    across(15).start()
-    pm = take(3)
-
-    def pack(r, a):
-        pas[r] = (pf[ablk(a), :] + pr0[ablk(a), :].astype(F32)).astype(BF16)
-
-    pack(2, a2)
-    pack(0, ap)
-    send(pas.at[2], pra.at[2], pm + 2, to_a2)
-    pack(1, am)
-    send(pas.at[0], pra.at[0], pm, to_ap)
-    mine = ablk(pa)
-    pf[mine, :] = pf[mine, :] + pr0[mine, :].astype(F32)
-    send(pas.at[1], pra.at[1], pm + 1, to_am)
-
-    hm = take(12)
-
-    def along_a(db, r):
-        return remote(cb.at[db * 3 + r], ra.at[r, db], hm + db * 3 + r, (to_ap, to_am, to_a2)[r])
+        up = grads[one].astype(F32) * jnp.minimum(total, 1).astype(F32)
+        down = grads[two].astype(F32) * jnp.maximum(total - 1, 0).astype(F32)
+        left = [turned[lax.div(one, BEAM)], turned[lax.div(two, BEAM)]]
+        return left, [up.astype(BF16), down.astype(BF16)]
 
     def own_clusters(db, carry):
         def value_of(da):
             c = lid((pa + 6 - da) % 4, (pb + 6 - db) % 4, core)
-            value = cluster(c)
-            across(db * 4 + da).wait_recv()
-            return value + rb[db * 4 + da].astype(F32)
+            left, right = halves(c, tab, hidt, gl)
+            left_s, right_s = halves(c, tab_s, hidt_s, gl_s)
+            return jnp.dot(
+                jnp.concatenate(left + left_s, axis=1),
+                jnp.concatenate(right + right_s, axis=0),
+                preferred_element_type=F32,
+            )
 
         cb[db * 3 + 2] = value_of(0).astype(BF16)
         cb[db * 3] = value_of(1).astype(BF16)
@@ -282,7 +320,8 @@
         along_a(db, 1).start()
         return carry
 
-    lax.fori_loop(0, 4, own_clusters, 0)
+    lax.fori_loop(0, 2, own_clusters, 0)
+    lax.fori_loop(3, 4, own_clusters, 0)
 
     outs = []
 
@@ -291,16 +330,7 @@
         ge[rows, :] = lax.dot_general(
             gh[rows, :], proj[...], (((1,), (1,)), ((), ())), preferred_element_type=F32
         )
-        if i > 0:
-            out_chunk(i - 1)
-
-    def out_chunk(i):
-        rows = pl.ds(256 * i, 256)
-        copy = pltpu.make_async_copy(ge.at[rows], ge_out.at[rows], ls.at[8 + i])
-        copy.start()
-        outs.append(copy)
-
-    enc_chunk(0)
+
     for r in range(3):
         landed(pra.at[r], pm + r)
     value = pf[mine, :] + pra[0].astype(F32) + pra[1].astype(F32) + pra[2].astype(F32)
@@ -311,18 +341,19 @@
         return pl.ds(pl.multiple_of(b * PIECE, 16), PIECE)
 
     pn = take(3)
-    enc_chunk(1)
+    lax.fori_loop(2, 3, own_clusters, 0)
     send(pbs.at[piece(b2)], prb.at[2], pn + 2, to_b2)
     send(pbs.at[piece(bp)], prb.at[0], pn, to_bp)
     send(pbs.at[piece(bm)], prb.at[1], pn + 1, to_bm)
     hn = take(3)
+    enc_chunk(0)
+    enc_chunk(1)
 
     def finish_a(db):
         for r in range(3):
             landed(ra.at[r, db], hm + db * 3 + r)
         return cf[db] + ra[0, db].astype(F32) + ra[1, db].astype(F32) + ra[2, db].astype(F32)
 
-    dbs[2] = finish_a(0).astype(BF16)
     for r in range(3):
         landed(prb.at[r], pn + r)
     spot_rows = pl.ds(pl.multiple_of(pa * ABLK + pb * PIECE, 16), PIECE)
@@ -330,15 +361,14 @@
     ez[...] = value.astype(BF16)
     zp[z] = value.astype(BF16)
     pz = take(NZ)
-    send(dbs.at[2], rbb.at[2], hn + 2, to_b2)
-    enc_chunk(2)
+    dbs[2] = finish_a(0).astype(BF16)
     for dz in (4, 3, 5, 2, 6, 1, 7):
         send(ez, zp.at[z], pz + dz, to_z[dz])
+    enc_chunk(2)
+    send(dbs.at[2], rbb.at[2], hn + 2, to_b2)
     dbs[0] = finish_a(1).astype(BF16)
     enc_chunk(3)
     send(dbs.at[0], rbb.at[0], hn, to_bp)
-    out_chunk(3)
-    cf[2] = finish_a(2)
     dbs[1] = finish_a(3).astype(BF16)
     for dz in range(1, NZ):
         landed(zp.at[(z + NZ - dz) % NZ], pz + dz)
@@ -350,42 +380,49 @@
     def spot(a, b):
         return po.at[pl.ds(pl.multiple_of((core * 4 + a) * ABLK + b * PIECE, 16), PIECE)]
 
-    def wide(a):
-        return po.at[pl.ds(pl.multiple_of((core * 4 + a) * ABLK, 16), ABLK)]
-
     po[pl.ds(pl.multiple_of((core * 4 + pa) * ABLK + pb * PIECE, 16), PIECE), :] = total.astype(BF16)
     g1 = take(3)
-    landed(rbb.at[2], hn + 2)
-    landed(rbb.at[0], hn)
+    g2 = take(12)
+    g3 = take(16)
+    along = [pb, bm, bp, b2]
+    hops = [am, ap, a2]
+
+    def outward(q):
+        held = spot(pa, along[q])
+        for r, device in enumerate((to_ap, to_am, to_a2)):
+            send(held, held, g2 + 3 * q + r, device)
+        send(held, held, g3 + q, sib)
+
+    held = spot(pa, pb)
     for r, device in enumerate((to_bp, to_bm, to_b2)):
-        send(spot(pa, pb), spot(pa, pb), g1 + r, device)
-    landed(rbb.at[1], hn + 1)
-    value = cf[2] + rbb[0].astype(F32) + rbb[1].astype(F32) + rbb[2].astype(F32)
+        send(held, held, g1 + r, device)
+    outward(0)
+    value = finish_a(2)
+    for r in (2, 0, 1):
+        landed(rbb.at[r], hn + r)
+    value = value + rbb[0].astype(F32) + rbb[1].astype(F32) + rbb[2].astype(F32)
     value = value.reshape(NZ, D // NZ, LB)
     ef[...] = value
     zs[...] = value.astype(BF16)
     hz = take(NZ)
-    landed(spot(pa, bm), g1)
+    for q in (1, 2, 3):
+        landed(spot(pa, along[q]), g1 + q - 1)
+        outward(q)
     for dz in (4, 3, 5, 2, 6, 1, 7):
         send(zs.at[(z + dz) % NZ], zr.at[dz], hz + dz, to_z[dz])
-    landed(spot(pa, bp), g1 + 1)
-    landed(spot(pa, b2), g1 + 2)
-    g2 = take(3)
-    g3 = take(4)
-    for r, device in enumerate((to_ap, to_am, to_a2)):
-        send(wide(pa), wide(pa), g2 + r, device)
-    send(wide(pa), wide(pa), g3, sib)
-    for r, a in enumerate((am, ap, a2)):
-        landed(wide(a), g2 + r)
-        send(wide(a), wide(a), g3 + 1 + r, sib)
+    for q in range(4):
+        for r in range(3):
+            held = spot(hops[r], along[q])
+            landed(held, g2 + 3 * q + r)
+            send(held, held, g3 + 4 + 3 * q + r, sib)
     for dz in range(1, NZ):
         landed(zr.at[dz], hz + dz)
     value = ef[z]
     for dz in range(1, NZ):
         value = value + zr[dz].astype(F32)
     gh_out[...] = value
-    for i in range(4):
-        landed(wide(pa), g3 + i)
+    for i in range(16):
+        landed(spot(pa, pb), g3 + i)
     for j in range(D // LB):
         copy = pltpu.make_async_copy(
             po.at[pl.ds(j * D, D)], gp_out.at[:, pl.ds(j * LB, LB)], ls.at[j])
@@ -395,10 +432,11 @@
         copy.wait_send()
 
     def drain(i, carry):
-        across(i).wait_send()
+        lend_gl(i).wait_send()
+        lend_gh(i).wait_send()
         return carry
 
-    lax.fori_loop(0, 16, drain, 0)
+    lax.fori_loop(0, NBLK, drain, 0)
 
     def drain_a(db, carry):
         for r in range(3):
@@ -411,24 +449,27 @@
     assert count[0] <= MESSAGES, count[0]
 
 
-MESSAGES = 128
+MESSAGES = 160
 
 
 def scratch():
     v = pltpu.VMEM
     return [
+        v((1, LB), jnp.int32), v((1, LB), jnp.int32), v((8, ROWS), jnp.int32),
         v((ROWS, D), BF16), v((D, D), BF16),
         v((32, SHARD, LB), BF16), v((NBLK, SB, 8), jnp.int32),
-        v((NBLK, SB, D), BF16), v((NBLK, D, SB), BF16),
-        v((D, ROWS), BF16), v((BEAM * LB, D), BF16), v((32, SB, LB), BF16),
-        v((ROWS, D), BF16), v((ROWS, D), F32),
-        v((16, D, LB), BF16), v((16, D, LB), BF16), v((12, D, LB), BF16), v((4, D, LB), F32),
+        v((NBLK, SB, D), BF16), v((NBLK, D, SB), BF16), v((NBLK, D, SB), BF16),
+        v((4, D, ROWS // 4), BF16), v((4, D, ROWS // 4), BF16),
+        v((BEAM * LB, D), BF16), v((32, SB, LB), BF16), v((32, SB, LB), BF16),
+        v((ROWS, D), BF16), v((ROWS, D), BF16),
+        v((12, D, LB), BF16), v((4, D, LB), F32),
         v((3, 4, D, LB), BF16), v((3, D, LB), BF16), v((3, D, LB), BF16),
         v((NZ, D // NZ, LB), F32), v((NZ, D // NZ, LB), BF16), v((NZ, D // NZ, LB), BF16),
-        v((CORE, LB), BF16), v((CORE, LB), BF16), v((CORE, LB), F32),
+        v((CORE, LB), F32),
         v((3, ABLK, LB), BF16), v((3, ABLK, LB), BF16),
         v((ABLK, LB), BF16), v((3, PIECE, LB), BF16),
         v((PIECE, LB), BF16), v((NZ, PIECE, LB), BF16), v((2 * CORE, LB), BF16),
+        pltpu.SMEM((1, 128), jnp.int32),
         pltpu.SemaphoreType.DMA((MESSAGES,)), pltpu.SemaphoreType.DMA((MESSAGES,)),
         pltpu.SemaphoreType.DMA((12,)),
     ]
@@ -441,22 +482,22 @@
     total = jnp.sum(match.astype(jnp.int32), axis=(1, 2))
     one = jnp.min(jnp.where(match, order, NBLK * BEAM - 1), axis=(1, 2))
     two = jnp.max(jnp.where(match, order, 0), axis=(1, 2))
-    tab = one + 32 * two + 1024 * total
+    tab = jnp.pad(one + 32 * two + 1024 * total, (0, 96)).reshape(1, 128)
     smem = pl.BlockSpec(memory_space=pltpu.SMEM)
     vmem = pl.BlockSpec(memory_space=pltpu.VMEM)
     anyspace = pl.BlockSpec(memory_space=pl.ANY)
     grad_enc, grad_proj, grad_head = pl.pallas_call(
         kernel,
         out_shape=(
-            jax.ShapeDtypeStruct((ROWS, D), F32),
+            pltpu.VMEM((ROWS, D), F32),
             jax.ShapeDtypeStruct((D, D), BF16),
             jax.ShapeDtypeStruct((D // NZ, LB), F32),
         ),
-        in_specs=[smem, smem, vmem, vmem, vmem, anyspace, anyspace, anyspace],
-        out_specs=(anyspace, anyspace, vmem),
+        in_specs=[smem, smem] + [pl.BlockSpec(memory_space=pltpu.HBM)] * 6,
+        out_specs=(vmem, anyspace, vmem),
         scratch_shapes=scratch(),
         compiler_params=pltpu.CompilerParams(
-            collective_id=0, has_side_effects=True, vmem_limit_bytes=60 << 20
+            collective_id=0, has_side_effects=True, vmem_limit_bytes=56 << 20
         ),
     )(
         shortlist.T, tab, weight_num.reshape(1, LB), weight_den.reshape(1, LB), positives.T,

time: 97.1 us -> 90.2 us (0.929)
  Pallas kernels: 88.9 us -> 83.8 us
  other arithmetic: 4.29 us -> 2.36 us
    pallas_call x1, Pallas kernels: 88.9 us -> 83.8 us  [shards(): pl.pallas_call(kernel, out_shape=(pltpu.VMEM((ROWS, D), F32), jax.ShapeDt...]
    convert_element_type x1, other arithmetic: 3 us -> 1.58 us  [shards(): return (grad_enc, grad_proj.astype(F32), grad_head.T)]
where the time goes in v4:
time: 90.2 us; the launch traced here: 90 us
  Pallas kernels  83.8 us (93%)
  local copies, waits for them, and re-layouts  3.21 us (4%)
  other arithmetic  2.36 us (3%)
    pallas_call x1, Pallas kernels, shards(): pl.pallas_call(kernel, out_shape=(pltpu.VMEM((ROWS, D), F32), jax.ShapeDt...  83.8 us
    unnamed x6, local copies, waits for them, and re-layouts  2.69 us

profile of v4, /device:TPU:1, one launch (start us, length us, event | category | flops | bytes accessed | tf_op | source)
XLA Modules:
  0.0 90.0 jit_solution(13643778220498448595)
XLA Ops:
  0.6 0.8 select_reduce_fusion
  1.4 0.5 pad_bitcast_fusion.tab
  1.9 83.8 %shard_map.94 = (f32[1024,768]{1,0:T(8,128)S(1)}, bf16[768,768]{1,0:T(8,128)(2,1)}, f32[96,128]{1,0:T(8,128)}) custom-call(s32[4,8]{1,0:T(4,128)} %bitcast.9, s32[1,128]{1,0:T(1,128)} %pad_bitcast_fusion.tab, s32[1,128]{1,0:T(1,128)} %bitcast.10, s32[1,128]{1,0:T(1,128)} %bitcast.11, s32[8,1024]{1,0:T(8,128)} %bitcast.8, bf16[1024,768]{1,0:T(8,128)(2,1)} %enc_in.1, ...), custom_call_target="tpu_custom_call" | custom-call | tf_op jit(solution)/shard_map/pallas_call | solution.py:489
  85.8 0.0 copy-start
  85.8 1.7 %copy.13 = f32[1024,768]{1,0:T(8,128)} copy(f32[1024,768]{1,0:T(8,128)S(1)} %get-tuple-element.12) | data formatting | bytes 6291456
  87.4 0.4 copy-done
  87.8 0.0 copy-start.1
  87.8 1.6 %convert_element_type.7 = f32[768,768]{1,0:T(8,128)} convert(bf16[768,768]{1,0:T(8,128)(2,1)S(1)} %copy-done) | non-fusion elementwise | flops 589824 | bytes 3538944 | tf_op jit(solution)/shard_map/convert_element_type | solution.py:506
  89.4 0.0 copy-done.1
  89.4 0.6 copy.14
  (2 shorter events, 0.0 us)
Async XLA Ops:
  85.8 2.1 %copy-start = (bf16[768,768]{1,0:T(8,128)(2,1)S(1)}, bf16[768,768]{1,0:T(8,128)(2,1)}, u32[]{:S(2)}) copy-start(bf16[768,768]{1,0:T(8,128)(2,1)} %get-tuple-element.7) | copy-start | bytes 3538948
  87.8 1.6 %copy-start.1 = (f32[96,128]{1,0:T(8,128)S(1)}, f32[96,128]{1,0:T(8,128)}, u32[]{:S(2)}) copy-start(f32[96,128]{1,0:T(8,128)} %get-tuple-element.8) | copy-start | bytes 147460

commit v5 on v4

--- a/solution.py
+++ b/solution.py
@@ -30,11 +30,11 @@
 
 
 def kernel(
-    sl, tab, num_in, den_in, post_in, enc_in, proj_in, head_in,
+    sl, num_in, den_in, post_in, enc_in, proj_in, head_in,
     ge, gp_out, gh_out,
     num, den, post, enc, proj, wl, pos, hid, hidt, hidt_s, enct, enct_s, w4, gl, gl_s, gh, gh_s,
     cb, cf, ra, dbs, rbb, ef, zs, zr,
-    pf, pas, pra, pbs, prb, ez, zp, po, tab_s,
+    pf, pas, pra, pbs, prb, ez, zp, po, tab, tab_s,
     ss, rs, ls,
 ):
     z = lax.axis_index("dp")
@@ -120,6 +120,17 @@
         send(hidt.at[pair], hidt_s.at[pair], share + 2 * i, sib)
         send(enct.at[i], enct_s.at[i], share + 2 * i + 1, sib)
 
+    def name_pairs(c, carry):
+        one, two, total = jnp.int32(0), jnp.int32(0), jnp.int32(0)
+        for p in range(NBLK * BEAM):
+            two = jnp.where(sl[p % BEAM, p // BEAM] == c, p, two)
+            total = total + jnp.where(sl[p % BEAM, p // BEAM] == c, 1, 0)
+        for p in reversed(range(NBLK * BEAM)):
+            one = jnp.where(sl[p % BEAM, p // BEAM] == c, p, one)
+        tab[0, c] = one + 32 * two + 1024 * total
+        return carry
+
+
     for load in loads[:6]:
         load.wait()
     pl.semaphore_wait(barrier, len(greeted))
@@ -142,8 +153,6 @@
         copy.wait_send()
     send(own, own, base, to_bp)
     send(own, own, base + 1, to_bm)
-    tabled = take()
-    send(tab, tab_s, tabled, sib)
     loads[6].wait()
     loads[7].wait()
     loads[8].wait()
@@ -188,8 +197,15 @@
         landed(held.at[top], base + 4 * j + 2)
         landed(held.at[bottom], base + 4 * j + 3)
         send(held, held, near + 12 + j, sib)
+        if j == 1:
+            lax.fori_loop(0, 32, name_pairs, 0)
+            for c in range(32, LB):
+                tab[0, c] = 0
     for i in range(16):
         landed(own, near + i)
+
+    tabled = take()
+    send(tab, tab_s, tabled, sib)
 
     place = lax.broadcasted_iota(jnp.int32, (SB, LB), 1)
 
@@ -323,8 +339,6 @@
     lax.fori_loop(0, 2, own_clusters, 0)
     lax.fori_loop(3, 4, own_clusters, 0)
 
-    outs = []
-
     def enc_chunk(i):
         rows = pl.ds(256 * i, 256)
         ge[rows, :] = lax.dot_general(
@@ -402,14 +416,14 @@
         landed(rbb.at[r], hn + r)
     value = value + rbb[0].astype(F32) + rbb[1].astype(F32) + rbb[2].astype(F32)
     value = value.reshape(NZ, D // NZ, LB)
+    zs[...] = value.astype(BF16)
     ef[...] = value
-    zs[...] = value.astype(BF16)
     hz = take(NZ)
+    for dz in (4, 3, 5, 2, 6, 1, 7):
+        send(zs.at[(z + dz) % NZ], zr.at[dz], hz + dz, to_z[dz])
     for q in (1, 2, 3):
         landed(spot(pa, along[q]), g1 + q - 1)
         outward(q)
-    for dz in (4, 3, 5, 2, 6, 1, 7):
-        send(zs.at[(z + dz) % NZ], zr.at[dz], hz + dz, to_z[dz])
     for q in range(4):
         for r in range(3):
             held = spot(hops[r], along[q])
@@ -421,13 +435,17 @@
     for dz in range(1, NZ):
         value = value + zr[dz].astype(F32)
     gh_out[...] = value
+
+    def widen(which):
+        for j in range(3):
+            lanes = pl.ds(pl.multiple_of((which * 3 + j) * LB, LB), LB)
+            rows = pl.ds(pl.multiple_of(which * CORE + j * D, 16), D)
+            gp_out[:, lanes] = po[rows, :].astype(F32)
+
+    widen(core)
     for i in range(16):
         landed(spot(pa, pb), g3 + i)
-    for j in range(D // LB):
-        copy = pltpu.make_async_copy(
-            po.at[pl.ds(j * D, D)], gp_out.at[:, pl.ds(j * LB, LB)], ls.at[j])
-        copy.start()
-        outs.append(copy)
+    widen(other)
     for copy in sent:
         copy.wait_send()
 
@@ -444,8 +462,6 @@
         return carry
 
     lax.fori_loop(0, 4, drain_a, 0)
-    for copy in outs:
-        copy.wait()
     assert count[0] <= MESSAGES, count[0]
 
 
@@ -469,41 +485,33 @@
         v((3, ABLK, LB), BF16), v((3, ABLK, LB), BF16),
         v((ABLK, LB), BF16), v((3, PIECE, LB), BF16),
         v((PIECE, LB), BF16), v((NZ, PIECE, LB), BF16), v((2 * CORE, LB), BF16),
-        pltpu.SMEM((1, 128), jnp.int32),
+        pltpu.SMEM((1, 128), jnp.int32), pltpu.SMEM((1, 128), jnp.int32),
         pltpu.SemaphoreType.DMA((MESSAGES,)), pltpu.SemaphoreType.DMA((MESSAGES,)),
         pltpu.SemaphoreType.DMA((12,)),
     ]
 
 
 def shards(enc, proj, head_weight, shortlist, positives, weight_num, weight_den):
-    ids = jnp.arange(32, dtype=jnp.int32)[:, None, None]
-    match = shortlist[None] == ids
-    order = jnp.arange(NBLK * BEAM, dtype=jnp.int32).reshape(1, NBLK, BEAM)
-    total = jnp.sum(match.astype(jnp.int32), axis=(1, 2))
-    one = jnp.min(jnp.where(match, order, NBLK * BEAM - 1), axis=(1, 2))
-    two = jnp.max(jnp.where(match, order, 0), axis=(1, 2))
-    tab = jnp.pad(one + 32 * two + 1024 * total, (0, 96)).reshape(1, 128)
     smem = pl.BlockSpec(memory_space=pltpu.SMEM)
     vmem = pl.BlockSpec(memory_space=pltpu.VMEM)
-    anyspace = pl.BlockSpec(memory_space=pl.ANY)
     grad_enc, grad_proj, grad_head = pl.pallas_call(
         kernel,
         out_shape=(
             pltpu.VMEM((ROWS, D), F32),
-            jax.ShapeDtypeStruct((D, D), BF16),
-            jax.ShapeDtypeStruct((D // NZ, LB), F32),
+            pltpu.VMEM((D, D), F32),
+            pltpu.VMEM((D // NZ, LB), F32),
         ),
-        in_specs=[smem, smem] + [pl.BlockSpec(memory_space=pltpu.HBM)] * 6,
-        out_specs=(vmem, anyspace, vmem),
+        in_specs=[smem] + [pl.BlockSpec(memory_space=pltpu.HBM)] * 6,
+        out_specs=(vmem, vmem, vmem),
         scratch_shapes=scratch(),
         compiler_params=pltpu.CompilerParams(
             collective_id=0, has_side_effects=True, vmem_limit_bytes=56 << 20
         ),
     )(
-        shortlist.T, tab, weight_num.reshape(1, LB), weight_den.reshape(1, LB), positives.T,
+        shortlist.T, weight_num.reshape(1, LB), weight_den.reshape(1, LB), positives.T,
         enc, proj, head_weight,
     )
-    return (grad_enc, grad_proj.astype(F32), grad_head.T)
+    return (grad_enc, grad_proj, grad_head.T)
 
 
 def solution(mesh):

time: 90.2 us -> 87 us (0.965)
  other arithmetic: 2.36 us -> 0 us
  Pallas kernels: 83.8 us -> 82.5 us
    convert_element_type x1 -> x0, other arithmetic: 1.58 us -> none  [shards(): return (grad_enc, grad_proj.astype(F32), grad_head.T)]
    pallas_call x1, Pallas kernels: 83.8 us -> 82.5 us  [shards(): pl.pallas_call(kernel, out_shape=(pltpu.VMEM((ROWS, D), F32), pltpu.VMEM(...]
    unnamed x6 -> x3, local copies, waits for them, and re-layouts: 2.69 us -> 3.69 us
where the time goes in v5:
time: 87 us; the launch traced here: 86.9 us
  Pallas kernels  82.5 us (95%)
  local copies, waits for them, and re-layouts  3.69 us (4%)
    pallas_call x1, Pallas kernels, shards(): pl.pallas_call(kernel, out_shape=(pltpu.VMEM((ROWS, D), F32), pltpu.VMEM(...  82.5 us
    unnamed x3, local copies, waits for them, and re-layouts  3.69 us

profile of v5, /device:TPU:1, one launch (start us, length us, event | category | flops | bytes accessed | tf_op | source)
XLA Modules:
  0.0 86.9 jit_solution(812502340563452852)
XLA Ops:
  0.6 82.5 %shard_map.94 = (f32[1024,768]{1,0:T(8,128)S(1)}, f32[768,768]{1,0:T(8,128)S(1)}, f32[96,128]{1,0:T(8,128)S(1)}) custom-call(s32[4,8]{1,0:T(4,128)} %bitcast.7, s32[1,128]{1,0:T(1,128)} %bitcast.8, s32[1,128]{1,0:T(1,128)} %bitcast.9, s32[8,1024]{1,0:T(8,128)} %bitcast.6, bf16[1024,768]{1,0:T(8,128)(2,1)} %enc_in.1, bf16[768,768]{1,0:T(8,128)(2,1)} %proj_in.1, ...), custom_call_target="tpu_custom_call" | custom-call | tf_op jit(solution)/shard_map/pallas_call | solution.py:497
  83.2 1.7 %copy.13 = f32[1024,768]{1,0:T(8,128)} copy(f32[1024,768]{1,0:T(8,128)S(1)} %get-tuple-element.9) | data formatting | bytes 6291456
  84.8 0.6 copy.15
  85.4 1.4 %copy.14 = f32[768,768]{1,0:T(8,128)} copy(f32[768,768]{1,0:T(8,128)S(1)} %get-tuple-element.10) | data formatting | bytes 4718592

commit v6 on v5

--- a/solution.py
+++ b/solution.py
@@ -225,16 +225,15 @@
             c = sl[k, b]
             for j in range(D // LB):
                 w4[k * LB:(k + 1) * LB, j * LB:(j + 1) * LB] = wl[c, j * LB:(j + 1) * LB, :]
-        rows = hid[b]
+        scores = lax.dot_general(
+            hid[b], w4[...], (((1,), (1,)), ((), ())), preferred_element_type=F32
+        )
         parts = []
         for k in range(BEAM):
             c = sl[k, b]
             ends = wl[c, D:SHARD, :].astype(F32)
             scale = ends[0:1] / ends[1:2]
-            logits = lax.dot_general(
-                rows, w4[k * LB:(k + 1) * LB, :], (((1,), (1,)), ((), ())),
-                preferred_element_type=F32,
-            )
+            logits = scores[:, k * LB:(k + 1) * LB]
             hit = wanted[:, 0:1] == place + k * LB
             for column in range(1, wanted.shape[1]):
                 hit = hit | (wanted[:, column:column + 1] == place + k * LB)
@@ -256,17 +255,20 @@
 
     lend_gl(NBLK - 1).start()
 
+    mid = D // 2
+
     def proj_part(left, right, j, n):
-        lanes = pl.ds(pl.multiple_of(core * (D // 2) + j * LB, 128), n * LB)
-        whole = jnp.concatenate([left[i] for i in range(4)], axis=1)
-        return jnp.dot(whole, right[:, lanes], preferred_element_type=F32)
-
-    value = proj_part(enct, gh, 0, 1)
+        rows = pl.ds(pl.multiple_of(core * mid, 16), mid)
+        whole = jnp.concatenate([left[i, rows, :] for i in range(4)], axis=1)
+        return jnp.dot(whole, right[:, j * LB:(j + n) * LB], preferred_element_type=F32)
+
+    value = proj_part(enct, gh, 0, 2)
     lend_gh(NBLK - 1).start()
-    pf[0:D, :] = value
-    value = proj_part(enct, gh, 1, 2)
-    pf[D:2 * D, :] = value[:, :LB]
-    pf[2 * D:3 * D, :] = value[:, LB:]
+    for j in range(2):
+        pf[j * mid:(j + 1) * mid, :] = value[:, j * LB:(j + 1) * LB]
+    value = proj_part(enct, gh, 2, 4)
+    for j in range(4):
+        pf[(j + 2) * mid:(j + 3) * mid, :] = value[:, j * LB:(j + 1) * LB]
     for i in range(4):
         landed(enct_s.at[i], share + 2 * i + 1)
 
@@ -275,9 +277,9 @@
         return carry
 
     lax.fori_loop(0, NBLK, arrive_gh, 0)
-    value = proj_part(enct_s, gh_s, 0, 3)
-    for j in range(3):
-        rows = slice(j * D, (j + 1) * D)
+    value = proj_part(enct_s, gh_s, 0, 6)
+    for j in range(6):
+        rows = slice(j * mid, (j + 1) * mid)
         pf[rows, :] = pf[rows, :] + value[:, j * LB:(j + 1) * LB]
 
     def ablk(a):
@@ -437,10 +439,10 @@
     gh_out[...] = value
 
     def widen(which):
-        for j in range(3):
-            lanes = pl.ds(pl.multiple_of((which * 3 + j) * LB, LB), LB)
-            rows = pl.ds(pl.multiple_of(which * CORE + j * D, 16), D)
-            gp_out[:, lanes] = po[rows, :].astype(F32)
+        for j in range(6):
+            rows = pl.ds(pl.multiple_of(which * CORE + j * mid, 16), mid)
+            spread_rows = pl.ds(pl.multiple_of(which * mid, 16), mid)
+            gp_out[spread_rows, j * LB:(j + 1) * LB] = po[rows, :].astype(F32)
 
     widen(core)
     for i in range(16):

time: 87 us -> 86 us (0.989)
  Pallas kernels: 82.5 us -> 81.6 us
    pallas_call x1, Pallas kernels: 82.5 us -> 81.6 us  [shards(): pl.pallas_call(kernel, out_shape=(pltpu.VMEM((ROWS, D), F32), pltpu.VMEM(...]
where the time goes in v6:
time: 86 us; the launch traced here: 85.9 us
  Pallas kernels  81.6 us (95%)
  local copies, waits for them, and re-layouts  3.69 us (4%)
    pallas_call x1, Pallas kernels, shards(): pl.pallas_call(kernel, out_shape=(pltpu.VMEM((ROWS, D), F32), pltpu.VMEM(...  81.6 us
    unnamed x3, local copies, waits for them, and re-layouts  3.69 us

profile of v6, /device:TPU:1, one launch (start us, length us, event | category | flops | bytes accessed | tf_op | source)
XLA Modules:
  0.0 85.9 jit_solution(11016783705084367509)
XLA Ops:
  0.6 81.6 %shard_map.94 = (f32[1024,768]{1,0:T(8,128)S(1)}, f32[768,768]{1,0:T(8,128)S(1)}, f32[96,128]{1,0:T(8,128)S(1)}) custom-call(s32[4,8]{1,0:T(4,128)} %bitcast.7, s32[1,128]{1,0:T(1,128)} %bitcast.8, s32[1,128]{1,0:T(1,128)} %bitcast.9, s32[8,1024]{1,0:T(8,128)} %bitcast.6, bf16[1024,768]{1,0:T(8,128)(2,1)} %enc_in.1, bf16[768,768]{1,0:T(8,128)(2,1)} %proj_in.1, ...), custom_call_target="tpu_custom_call" | custom-call | tf_op jit(solution)/shard_map/pallas_call | solution.py:499
  82.2 1.7 %copy.13 = f32[1024,768]{1,0:T(8,128)} copy(f32[1024,768]{1,0:T(8,128)S(1)} %get-tuple-element.9) | data formatting | bytes 6291456
  83.9 0.6 copy.15
  84.5 1.4 %copy.14 = f32[768,768]{1,0:T(8,128)} copy(f32[768,768]{1,0:T(8,128)S(1)} %get-tuple-element.10) | data formatting | bytes 4718592

commit v7 on v6

--- a/solution.py
+++ b/solution.py
@@ -340,6 +340,7 @@
 
     lax.fori_loop(0, 2, own_clusters, 0)
     lax.fori_loop(3, 4, own_clusters, 0)
+    lax.fori_loop(2, 3, own_clusters, 0)
 
     def enc_chunk(i):
         rows = pl.ds(256 * i, 256)
@@ -350,14 +351,13 @@
     for r in range(3):
         landed(pra.at[r], pm + r)
     value = pf[mine, :] + pra[0].astype(F32) + pra[1].astype(F32) + pra[2].astype(F32)
+    pbs[...] = value.astype(BF16)
     pf[mine, :] = value
-    pbs[...] = value.astype(BF16)
 
     def piece(b):
         return pl.ds(pl.multiple_of(b * PIECE, 16), PIECE)
 
     pn = take(3)
-    lax.fori_loop(2, 3, own_clusters, 0)
     send(pbs.at[piece(b2)], prb.at[2], pn + 2, to_b2)
     send(pbs.at[piece(bp)], prb.at[0], pn, to_bp)
     send(pbs.at[piece(bm)], prb.at[1], pn + 1, to_bm)

time: 86 us -> 86 us (level)
  no operation moved by 1% of the time
where the time goes in v7:
time: 86 us; the launch traced here: 85.9 us
  Pallas kernels  81.6 us (95%)
  local copies, waits for them, and re-layouts  3.69 us (4%)
    pallas_call x1, Pallas kernels, shards(): pl.pallas_call(kernel, out_shape=(pltpu.VMEM((ROWS, D), F32), pltpu.VMEM(...  81.6 us
    unnamed x3, local copies, waits for them, and re-layouts  3.69 us

profile of v7, /device:TPU:1, one launch (start us, length us, event | category | flops | bytes accessed | tf_op | source)
XLA Modules:
  0.0 85.9 jit_solution(13912358053730084674)
XLA Ops:
  0.6 81.6 %shard_map.94 = (f32[1024,768]{1,0:T(8,128)S(1)}, f32[768,768]{1,0:T(8,128)S(1)}, f32[96,128]{1,0:T(8,128)S(1)}) custom-call(s32[4,8]{1,0:T(4,128)} %bitcast.7, s32[1,128]{1,0:T(1,128)} %bitcast.8, s32[1,128]{1,0:T(1,128)} %bitcast.9, s32[8,1024]{1,0:T(8,128)} %bitcast.6, bf16[1024,768]{1,0:T(8,128)(2,1)} %enc_in.1, bf16[768,768]{1,0:T(8,128)(2,1)} %proj_in.1, ...), custom_call_target="tpu_custom_call" | custom-call | tf_op jit(solution)/shard_map/pallas_call | solution.py:499
  82.2 1.7 %copy.13 = f32[1024,768]{1,0:T(8,128)} copy(f32[1024,768]{1,0:T(8,128)S(1)} %get-tuple-element.9) | data formatting | bytes 6291456
  83.9 0.6 copy.15
  84.5 1.4 %copy.14 = f32[768,768]{1,0:T(8,128)} copy(f32[768,768]{1,0:T(8,128)S(1)} %get-tuple-element.10) | data formatting | bytes 4718592
